TPU v7x, 512 devices: a whole 4x8x8 slice. The times are simulated.
512 devices in a mesh: chan: 4 (over x), pair: 128 (over y, z, core).
Axes of the slice: x: 4, y: 8, z: 8, core: 2. Of those that a mesh axis runs over, the one named last changes fastest.
Arguments:
- visibility: bfloat16 [4, 65536, 256], P('chan', 'pair'), may hold values from -6 to 6
- pair_counts: int32 [65536], P('pair'), may hold values from 1 to 4
- owner_ids: int32 [65536, 1], P('pair'), may hold values from 0 to 127; in each aligned block of 512 rows (0 to 511, 512 to 1023, ...) at most 12 rows name the same one
- slot_ids: int32 [65536], P('pair'), may hold values from 0 to 127
- beam: float32 [4, 2, 2, 16384, 1024], P('chan', None, None, 'pair'), may hold values from -0.125 to 0.125
Outputs:
- modes: float32 [4, 1024, 2, 2, 64], P('chan', 'pair')
- mode_power: float32 [1024, 2], P('pair')
Inputs may be any that keep to these rules, and one draw needn't show every extreme that they name: `owner_ids`: among the 512 feed pairs of one device, no owner is named more than 12 times, a bound that some block reaches.
All inputs are finite; a program needn't handle non-finite values.
Results may differ from a plain program's by a relative error of at most 0.0017.
Values may be sent and summed in bfloat16 or wider, within the bound.
A program may use at most 64 MiB of HBM per device.

v0:
```python
import jax
import jax.numpy as jnp
from jax import lax
from jax.sharding import PartitionSpec as P


def per_device(visibility, pair_counts, owner_ids, slot_ids, beam):
    peers = lax.axis_size("pair")
    pair_rows = pair_counts.shape[0]
    capacity = 2 * pair_rows // peers + 4
    owner = owner_ids[:, 0]
    order = jnp.argsort(owner, stable=True)
    sorted_owner = owner[order]
    owner_list = jnp.arange(peers, dtype=jnp.int32)
    first_at = jnp.searchsorted(sorted_owner, owner_list, side="left")
    last_at = jnp.searchsorted(sorted_owner, owner_list, side="right")
    ranks = jnp.arange(capacity, dtype=jnp.int32)
    valid = ranks[None, :] < (last_at - first_at)[:, None]
    where_at = jnp.clip(first_at[:, None] + ranks[None, :], 0, pair_rows - 1)
    picked = order[where_at]
    weights = jnp.where(valid, pair_counts[picked], 0)
    offsets = jnp.where(valid, slot_ids[picked], 0)
    rows = visibility[0][picked]
    weighted = (rows.astype(jnp.float32) * weights[:, :, None].astype(jnp.float32)).astype(
        jnp.bfloat16
    )
    got_rows, got_offsets, got_weights = (
        lax.all_to_all(weighted, "pair", split_axis=0, concat_axis=0, tiled=True),
        lax.all_to_all(offsets, "pair", split_axis=0, concat_axis=0, tiled=True),
        lax.all_to_all(weights, "pair", split_axis=0, concat_axis=0, tiled=True),
    )
    columns = got_rows.shape[2]
    got_rows = got_rows.reshape(peers * capacity, columns)
    got_offsets = got_offsets.reshape(peers * capacity)
    got_weights = got_weights.reshape(peers * capacity).astype(jnp.float32)
    beam_local = beam[0]
    mwin = beam_local.shape[0]
    base_dev = beam_local.shape[2]
    sets = columns // (2 * mwin)
    matches = jnp.arange(base_dev, dtype=jnp.int32)[:, None] == got_offsets[None, :]
    numer = jnp.dot(matches.astype(jnp.bfloat16), got_rows, preferred_element_type=jnp.float32)
    denom = jnp.sum(jnp.where(matches, got_weights[None, :], 0.0), axis=1)
    stacked = numer / jnp.maximum(denom, 1.0)[:, None]
    stacked = stacked.reshape(base_dev, mwin, 2 * sets)
    real_part = stacked[:, :, :sets]
    imag_part = stacked[:, :, sets:]
    swapped = jnp.concatenate([imag_part, -real_part], axis=2)
    right = jnp.stack([stacked, swapped], axis=0)
    amplitudes = lax.psum_scatter(
        jnp.einsum(
            "mrbk,rbmc->kmc",
            beam_local,
            right,
            precision=lax.Precision.HIGHEST,
            preferred_element_type=jnp.float32,
        ),
        "pair",
        scatter_dimension=0,
        tiled=True,
    )
    power_local = jnp.sum(amplitudes * amplitudes, axis=2)
    total_power = lax.psum(power_local, "chan")
    mode_power = total_power / (lax.axis_size("chan") * sets)
    shaped = amplitudes.reshape(amplitudes.shape[0], mwin, 2, sets)
    return (shaped[None], mode_power)


def solution(mesh):
    in_specs = (
        P("chan", "pair", None),
        P("pair"),
        P("pair", None),
        P("pair"),
        P("chan", None, None, "pair", None),
    )
    out_specs = (P("chan", "pair", None, None, None), P("pair", None))
    return jax.shard_map(
        per_device, mesh=mesh, in_specs=in_specs, out_specs=out_specs, check_vma=False
    )
```

profile of v0, /device:TPU:1, one launch (start us, length us, event | category | flops | bytes accessed | tf_op | source)
XLA Modules:
  0.0 372.7 jit_solution(15409937679191300736)
XLA Ops:
  7.2 4.6 %sort.17 = (s32[512]{0:T(512)}, s32[512]{0:T(512)S(1)}) sort(s32[512]{0:T(512)} %bitcast.24, s32[512]{0:T(512)S(1)} %iota.29), dimensions={0}, to_apply=%region_0.0 | sort | flops 4608 | bytes 8192 | tf_op jit(solution)/shard_map/jit(argsort)/sort | solution.py:12
  11.8 3.6 gather_fusion.2
  15.4 13.3 %while.49 = (s32[]{:T(128)}, u32[128]{0:T(128)S(1)}, u32[128]{0:T(128)S(1)}, s32[512]{0:T(512)S(1)}, s32[]{:T(128)}, /*index=5*/s32[]{:T(128)}, s32[]{}) while((s32[]{:T(128)}, u32[128]{0:T(128)S(1)}, u32[128]{0:T(128)S(1)}, s32[512]{0:T(512)S(1)}, s32[]{:T(128)}, /*index=5*/s32[]{:T(128)}, s32[]{}) %tuple.71), condition=%wide.region_4.5_spmd.clone, body=%wide.region_3.4_spmd.clone.sunk | while | flops 2692 | bytes 10340 | solution.py:15
  15.5 1.3 gather_fusion.1
  16.8 1.3 gather_fusion.1
  18.1 1.3 gather_fusion.1
  29.0 9.5 %gather_fusion.3 = s32[1536]{0:T(1024)S(1)} fusion(s32[512]{0:T(512)S(1)} %get-tuple-element.133, s32[2048]{0:T(1024)S(1)} %pad_clamp_fusion.3), kind=kCustom, calls=%fused_computation.3 | custom fusion | bytes 18432 | tf_op jit(solution)/shard_map/gather | solution.py:20
  39.2 9.5 %gather_fusion.6 = s32[1536]{0:T(1024)S(1)} fusion(s32[512]{0:T(512)S(1)} %copy-done.1, s32[2048]{0:T(1024)S(1)} %pad_clamp_fusion.2), kind=kCustom, calls=%fused_computation.6 | custom fusion | bytes 18432 | tf_op jit(solution)/shard_map/gather | solution.py:21
  48.8 13.4 %while.48 = (s32[]{:T(128)}, u32[128]{0:T(128)S(1)}, u32[128]{0:T(128)S(1)}, s32[512]{0:T(512)S(1)}, s32[]{:T(128)}, /*index=5*/s32[]{:T(128)}, s32[]{}) while((s32[]{:T(128)}, u32[128]{0:T(128)S(1)}, u32[128]{0:T(128)S(1)}, s32[512]{0:T(512)S(1)}, s32[]{:T(128)}, /*index=5*/s32[]{:T(128)}, s32[]{}) %tuple.79), condition=%wide.region_2.3_spmd.clone, body=%wide.region_1.2_spmd.clone.sunk | while | flops 2692 | bytes 10340 | solution.py:16
  62.2 9.5 %gather_fusion.4 = s32[1536]{0:T(1024)S(1)} fusion(s32[512]{0:T(512)S(1)} %copy-done.2, s32[2048]{0:T(1024)S(1)} %pad_clamp_fusion.2), kind=kCustom, calls=%fused_computation.4 | custom fusion | bytes 18432 | tf_op jit(solution)/shard_map/gather | solution.py:22
  72.5 18.4 %all-to-all-start = ((s32[128,1,12]{2,1,0:T(1,128)}), s32[128,1,12]{2,1,0:T(1,128)S(1)}, u32[]{:S(2)}, u32[]{:S(2)}) async-start(s32[128,1,12]{2,1,0:T(1,128)} %bitcast.1), calls=%async_computation | async-start | bytes 131072 | tf_op jit(solution)/shard_map/all_to_all | solution.py:29
  91.1 4.8 %gather_fusion.5 = bf16[1536,256]{1,0:T(8,128)(2,1)S(1)} fusion(bf16[512,256]{1,0:T(8,128)(2,1)S(1)} %bitcast.26, s32[2048]{0:T(1024)S(1)} %pad_clamp_fusion.2), kind=kCustom, calls=%fused_computation.5 | custom fusion | bytes 1579008 | tf_op jit(solution)/shard_map/gather | solution.py:23
  95.9 1.5 reshape.237
  97.4 5.1 %all-to-all-done = s32[128,1,12]{2,1,0:T(1,128)S(1)} async-done(((s32[128,1,12]{2,1,0:T(1,128)}), s32[128,1,12]{2,1,0:T(1,128)S(1)}, u32[]{:S(2)}, u32[]{:S(2)}) %all-to-all-start) | async-done | bytes 6176 | tf_op jit(solution)/shard_map/all_to_all | solution.py:29
  102.5 8.6 %all-to-all-start.2 = ((s32[128,1,12]{2,1,0:T(1,128)}), s32[128,1,12]{2,1,0:T(1,128)S(1)}, u32[]{:S(2)}, u32[]{:S(2)}) async-start(s32[128,1,12]{2,1,0:T(1,128)} %bitcast.3), calls=%async_computation.2 | async-start | bytes 131072 | tf_op jit(solution)/shard_map/all_to_all | solution.py:30
  111.1 2.9 multiply_convert_fusion
  114.1 8.6 %all-to-all-done.2 = s32[128,1,12]{2,1,0:T(1,128)S(1)} async-done(((s32[128,1,12]{2,1,0:T(1,128)}), s32[128,1,12]{2,1,0:T(1,128)S(1)}, u32[]{:S(2)}, u32[]{:S(2)}) %all-to-all-start.2) | async-done | bytes 6176 | tf_op jit(solution)/shard_map/all_to_all | solution.py:30
  122.7 5.7 %all-to-all-start.1 = ((bf16[128,12,256]{2,1,0:T(8,128)(2,1)}), bf16[128,12,256]{2,1,0:T(8,128)(2,1)S(1)}, u32[]{:S(2)}, u32[]{:S(2)}) async-start(bf16[128,12,256]{2,1,0:T(8,128)(2,1)} %multiply_convert_fusion), calls=%async_computation.1 | async-start | bytes 2097152 | tf_op jit(solution)/shard_map/all_to_all | solution.py:28
  130.5 28.4 %all-to-all-done.1 = bf16[128,12,256]{2,1,0:T(8,128)(2,1)S(1)} async-done(((bf16[128,12,256]{2,1,0:T(8,128)(2,1)}), bf16[128,12,256]{2,1,0:T(8,128)(2,1)S(1)}, u32[]{:S(2)}, u32[]{:S(2)}) %all-to-all-start.1) | async-done | bytes 786464 | tf_op jit(solution)/shard_map/all_to_all | solution.py:28
  160.0 1.4 convolution_divide_fusion
  162.8 1.3 copy.33
  164.2 1.3 dynamic-slice
  166.1 189.2 %all-reduce.3.cloned.1.call-done = f32[1024,2,128]{2,1,0:T(2,128)} async-done(((f32[1024,2,128]{2,1,0:T(2,128)}), f32[1024,2,128]{2,1,0:T(2,128)}) %all-reduce.3.cloned.1.call-update) | async-done | bytes 1048592
  356.8 8.4 %psum.7 = f32[8,2]{1,0:T(8,128)S(1)} all-reduce(f32[8,2]{1,0:T(8,128)S(1)} %get-tuple-element.194), channel_id=1, replica_groups=mesh['chan'=4,'pair'=128] {'chan'}, use_global_device_ids=true, to_apply=%region_8.9 | all-reduce | flops 16 | bytes 128 | tf_op jit(solution)/shard_map/psum | solution.py:62
  (124 shorter events, 30.8 us)
Async XLA Ops:
  7.2 154.4 %copy-start = (f32[1,2,2,128,1024]{4,3,2,1,0:T(8,128)S(1)}, f32[1,2,2,128,1024]{4,3,2,1,0:T(8,128)}, u32[]{:S(2)}) copy-start(f32[1,2,2,128,1024]{4,3,2,1,0:T(8,128)} %param.13) | copy-start | bytes 6291460
  38.5 0.7 copy-start.1
  48.7 13.5 %copy-start.2 = (s32[512]{0:T(512)S(1)}, s32[512]{0:T(512)}, u32[]{:S(2)}) copy-start(s32[512]{0:T(512)} %param.12) | copy-start | bytes 6148
  71.7 19.5 %copy-start.3 = (bf16[1,512,256]{2,1,0:T(8,128)(2,1)S(1)}, bf16[1,512,256]{2,1,0:T(8,128)(2,1)}, u32[]{:S(2)}) copy-start(bf16[1,512,256]{2,1,0:T(8,128)(2,1)} %param.9) | copy-start | bytes 786436
  72.5 30.0 %all-to-all-start = ((s32[128,1,12]{2,1,0:T(1,128)}), s32[128,1,12]{2,1,0:T(1,128)S(1)}, u32[]{:S(2)}, u32[]{:S(2)}) async-start(s32[128,1,12]{2,1,0:T(1,128)} %bitcast.1), calls=%async_computation | async-start | bytes 131072 | tf_op jit(solution)/shard_map/all_to_all | solution.py:29
  102.5 20.2 %all-to-all-start.2 = ((s32[128,1,12]{2,1,0:T(1,128)}), s32[128,1,12]{2,1,0:T(1,128)S(1)}, u32[]{:S(2)}, u32[]{:S(2)}) async-start(s32[128,1,12]{2,1,0:T(1,128)} %bitcast.3), calls=%async_computation.2 | async-start | bytes 131072 | tf_op jit(solution)/shard_map/all_to_all | solution.py:30
  122.7 36.2 %all-to-all-start.1 = ((bf16[128,12,256]{2,1,0:T(8,128)(2,1)}), bf16[128,12,256]{2,1,0:T(8,128)(2,1)S(1)}, u32[]{:S(2)}, u32[]{:S(2)}) async-start(bf16[128,12,256]{2,1,0:T(8,128)(2,1)} %multiply_convert_fusion), calls=%async_computation.1 | async-start | bytes 2097152 | tf_op jit(solution)/shard_map/all_to_all | solution.py:28
  128.4 226.9 %all-reduce.3.cloned.1.call-start = ((), (), s32[]{:S(2)}) async-start(), calls=%async_computation.3 | async-start | bytes 2097152
Sparse Core Ops, SparseCore 0:
  164.3 190.9 all-reduce.2
where the time goes:
time: 376 us; the launch traced here: 373 us
  waiting for transfers between devices  231 us (61%)
  local copies, waits for them, and re-layouts  70.5 us (19%)
  starting transfers between devices  33 us (9%)
  between operations  15 us (4%)
  other arithmetic  11 us (3%)
  blocking collectives  8.37 us (2%)
    unnamed x2, waiting for transfers between devices  189 us
    all_to_all x1, waiting for transfers between devices, per_device(): lax.all_to_all(weighted, 'pair', split_axis=0, concat_axis=0, tiled=True)  28.4 us
    all_to_all x1, starting transfers between devices, per_device(): lax.all_to_all(offsets, 'pair', split_axis=0, concat_axis=0, tiled=True)  18.4 us
    gather x10, local copies, waits for them, and re-layouts, per_device(): last_at = jnp.searchsorted(sorted_owner, owner_list, side='right')  12.7 us
    gather x10, local copies, waits for them, and re-layouts, per_device(): first_at = jnp.searchsorted(sorted_owner, owner_list, side='left')  12.7 us
    gather x3, local copies, waits for them, and re-layouts, per_device(): weights = jnp.where(valid, pair_counts[picked], 0)  9.67 us
    gather x2, local copies, waits for them, and re-layouts, per_device(): picked = order[where_at]  9.58 us
    gather x2, local copies, waits for them, and re-layouts, per_device(): offsets = jnp.where(valid, slot_ids[picked], 0)  9.58 us
  transfers between devices with their start and end apart: 4, of which 4 were waited for; matrix products, arithmetic and copies ran while one was open for 3% of the time, Pallas kernels for 0%

commit v1 on v0

v1 whole, which is shorter than its diff:
```python
import functools

import jax
import jax.numpy as jnp
from jax import lax
from jax.experimental import pallas as pl
from jax.experimental.pallas import tpu as pltpu
from jax.sharding import PartitionSpec as P

MESH = pl.DeviceIdType.MESH
F32, BF16, I32, I16 = jnp.float32, jnp.bfloat16, jnp.int32, jnp.int16


def iota(shape, axis):
    return lax.broadcasted_iota(I32, shape, axis)


def dot(a, b):
    return jnp.dot(a, b, preferred_element_type=F32)


def dot_nt(a, b):
    return lax.dot_general(a, b, (((1,), (1,)), ((), ())), preferred_element_type=F32)


def body(
    n, nchan, sets,
    owner_hbm, slot_hbm, count_hbm, vis_hbm, beam_hbm,
    modes_ref, power_ref,
    owner_ref, slot_ref, count_ref, vis_ref,
    send, recv, meta_send, meta_recv,
    beam_buf, beam_hi, beam_lo, hot_a, hot_b, inv_denom,
    part, core_recv, send2, recv2, scale_send, scale_recv, pow_send, pow_recv,
    in_sem, beam_sem, meta_s, meta_r, data_s, data_r, core_s, core_r, red_s, red_r, scale_s, scale_r, pow_s, pow_r,
):
    chan = lax.axis_index("chan")
    me = lax.axis_index("pair")
    chips = n // 2
    chip, core = me // 2, me % 2
    rows, columns = vis_ref.shape
    step_chips = min(8, chips)

    loads = [
        pltpu.make_async_copy(src, dst, in_sem.at[i])
        for i, (src, dst) in enumerate((
            (owner_hbm, owner_ref), (slot_hbm, slot_ref), (count_hbm, count_ref), (vis_hbm, vis_ref),
        ))
    ]
    for load in loads:
        load.start()
    beam_copy = pltpu.make_async_copy(beam_hbm, beam_buf, beam_sem)
    beam_copy.start()

    barrier = pltpu.get_barrier_semaphore()

    def greet(i, carry):
        peer = lax.rem(me + i, n)
        pl.semaphore_signal(barrier, inc=1, device_id={"chan": chan, "pair": peer}, device_id_type=MESH)
        return carry

    lax.fori_loop(1, n, greet, 0)
    for i in range(1, nchan):
        peer = lax.rem(chan + i, nchan)
        pl.semaphore_signal(barrier, inc=1, device_id={"chan": peer, "pair": me}, device_id_type=MESH)

    for load in loads:
        load.wait()

    owner = owner_ref[...]
    count = count_ref[...].astype(F32)
    slot = slot_ref[...].astype(F32)
    own_hot = jnp.where(iota((n, rows), 0) == owner, 1.0, 0.0).astype(BF16)
    before = jnp.where(iota((rows, rows), 0) < iota((rows, rows), 1), 1.0, 0.0).astype(BF16)
    rank = jnp.sum(own_hot.astype(F32) * dot(own_hot, before), axis=0, keepdims=True).astype(I32)

    lane_hit = iota((128, rows), 0) == rank
    by_slot = jnp.where(lane_hit, slot, 0.0).astype(BF16)
    by_count = jnp.where(lane_hit, count * 128.0, 0.0).astype(BF16)
    meta = dot_nt(own_hot, by_slot) + dot_nt(own_hot, by_count)
    meta_send[...] = meta.reshape(n, 1, 128)

    target_a = jnp.where(rank < 8, owner * 8 + rank, -1)
    target_b = jnp.where(rank >= 8, owner * 8 + rank - 8, -1)
    step_owners = min(16, n)
    step_rows = step_owners * 8

    def pack(i, carry):
        place = iota((step_rows, rows), 0) + i * step_rows
        pick_a = jnp.where(place == target_a, count, 0.0).astype(BF16)
        pick_b = jnp.where((place & -5) == target_b, count, 0.0).astype(BF16)
        vis = vis_ref[...]
        got_a = dot(pick_a, vis)
        got_b = dot(pick_b, vis)
        low = (iota((step_rows, 128), 0) & 4) == 0
        mixed = jnp.where(low, got_b[:, :128], got_b[:, 128:])
        at = pl.ds(i * step_owners, step_owners)
        send[at, 0] = got_a[:, :128].reshape(step_owners, 8, 128).astype(BF16)
        send[at, 1] = got_a[:, 128:].reshape(step_owners, 8, 128).astype(BF16)
        send[at, 2] = mixed.reshape(step_owners, 8, 128).astype(BF16)
        return carry

    lax.fori_loop(0, n // step_owners, pack, 0)

    pl.semaphore_wait(barrier, n - 1 + nchan - 1)

    own_meta = pltpu.make_async_copy(meta_send.at[me], meta_recv.at[me], meta_r)
    own_meta.start()
    own_data = pltpu.make_async_copy(send.at[me], recv.at[me], data_r)
    own_data.start()

    def send_meta(i, carry):
        peer = lax.rem(me + i, n)
        pltpu.make_async_remote_copy(
            meta_send.at[peer], meta_recv.at[me], meta_s, meta_r,
            device_id={"chan": chan, "pair": peer}, device_id_type=MESH).start()
        return carry

    lax.fori_loop(1, n, send_meta, 0)

    def send_data(i, carry):
        peer = lax.rem(me + i, n)
        pltpu.make_async_remote_copy(
            send.at[peer], recv.at[me], data_s, data_r,
            device_id={"chan": chan, "pair": peer}, device_id_type=MESH).start()
        return carry

    lax.fori_loop(1, n, send_data, 0)

    beam_copy.wait()
    mwin, modes = beam_buf.shape[0], beam_buf.shape[3]
    base = beam_buf.shape[2]
    for m in range(mwin):
        for r in range(2):
            def split(i, carry, m=m, r=r):
                at = pl.ds(i * 16, 16)
                full = beam_buf[m, r, at, :]
                high = full.astype(BF16)
                beam_hi[m, pl.ds(r * base + i * 16, 16), :] = high
                beam_lo[m, pl.ds(r * base + i * 16, 16), :] = (full - high.astype(F32)).astype(BF16)
                return carry

            lax.fori_loop(0, base // 16, split, 0)

    pltpu.make_async_copy(meta_recv, meta_recv, meta_r).wait()
    code = jnp.transpose(meta_recv[...].reshape(n, 128))[:16]
    weight = jnp.floor(code * (1.0 / 128.0))
    place = code - weight * 128.0
    both = jnp.concatenate([place, weight], axis=0).astype(BF16)
    spread = dot(both, jnp.where(iota((n, n * 8), 0) == iota((n, n * 8), 1) // 8, 1.0, 0.0).astype(BF16))
    ranks = iota((16, n * 8), 0)
    in_message = iota((16, n * 8), 1) & 7
    at_a = ranks == in_message
    at_b = ranks == 8 + (in_message & 3)

    def flat(values, mask):
        return jnp.sum(jnp.where(mask, values, 0.0), axis=0, keepdims=True)

    slot_a, slot_b = flat(spread[:16], at_a), flat(spread[:16], at_b)
    weight_a, weight_b = flat(spread[16:], at_a), flat(spread[16:], at_b)
    bases = iota((base, n * 8), 0).astype(F32)
    first = (iota((base, n * 8), 1) & 4) == 0
    hit_a = jnp.where(bases == slot_a, 1.0, 0.0)
    hit_b = jnp.where(bases == slot_b, 1.0, 0.0)
    hot_a[...] = hit_a.astype(BF16)
    hot_b[:base] = jnp.where(first, hit_b, 0.0).astype(BF16)
    hot_b[base:] = jnp.where(first, 0.0, hit_b).astype(BF16)
    denom = jnp.sum(hit_a * weight_a + jnp.where(first, hit_b, 0.0) * weight_b, axis=1, keepdims=True)
    inv_denom[...] = jnp.broadcast_to(jnp.maximum(denom, 1.0), (base, 128))

    pltpu.make_async_copy(recv, recv, data_r).wait()

    rows_0 = recv[:, 0].reshape(n * 8, 128)
    rows_1 = recv[:, 1].reshape(n * 8, 128)
    rows_2 = recv[:, 2].reshape(n * 8, 128)
    late = dot(hot_b[...], rows_2)
    numer = (dot(hot_a[...], rows_0) + late[:base], dot(hot_a[...], rows_1) + late[base:])
    sign = jnp.where(iota((base, 128), 1) < sets, 1.0, -1.0)
    for m in range(mwin):
        stacked = numer[m] / inv_denom[...]
        swapped = jnp.concatenate([stacked[:, sets:], stacked[:, :sets]], axis=1) * sign
        right = jnp.concatenate([jnp.transpose(stacked), jnp.transpose(swapped)], axis=1)
        high = right.astype(BF16)
        low = (right - high.astype(F32)).astype(BF16)
        step_modes = min(256, modes)

        def project(i, carry, m=m, high=high, low=low):
            at = pl.ds(pl.multiple_of(i * step_modes, step_modes), step_modes)
            hi = beam_hi[m, :, at]
            lo = beam_lo[m, :, at]
            sums = dot(high, hi) + (dot(low, hi) + dot(high, lo))
            blocks = jnp.transpose(sums).reshape(step_modes // 16, 2, 8, 128)
            part[pl.ds(i * (step_modes // 16), step_modes // 16), :, :, pl.ds(m * 128, 128)] = blocks
            return carry

        lax.fori_loop(0, modes // step_modes, project, 0)

    to_core = pltpu.make_async_remote_copy(
        part.at[:, 1 - core], core_recv, core_s, core_r,
        device_id={"chan": chan, "pair": me + 1 - 2 * core}, device_id_type=MESH)
    to_core.start()
    to_core.wait_recv()
    summed = part[:, core] + core_recv[...]
    core_recv[...] = summed
    peak = jnp.max(jnp.abs(summed), axis=(0, 1, 2), keepdims=True).reshape(1, 1)
    peak = jnp.maximum(peak, 1e-30)
    scale_send[...] = jnp.broadcast_to(peak * (1.0 / 32000.0), (1, 128))
    factor = jnp.broadcast_to(32000.0 / peak, (8, columns))

    def code_sums(i, carry):
        scaled = core_recv[pl.ds(i * step_chips, step_chips)] * factor
        send2[pl.ds(i * step_chips, step_chips)] = jnp.round(scaled).astype(I32).astype(I16)
        return carry

    lax.fori_loop(0, chips // step_chips, code_sums, 0)

    own_scale = pltpu.make_async_copy(scale_send, scale_recv.at[chip], scale_r)
    own_scale.start()
    own_red = pltpu.make_async_copy(send2.at[chip], recv2.at[chip], red_r)
    own_red.start()

    def send_red(i, carry):
        peer = lax.rem(chip + i, chips)
        pltpu.make_async_remote_copy(
            scale_send, scale_recv.at[chip], scale_s, scale_r,
            device_id={"chan": chan, "pair": peer * 2 + core}, device_id_type=MESH).start()
        pltpu.make_async_remote_copy(
            send2.at[peer], recv2.at[chip], red_s, red_r,
            device_id={"chan": chan, "pair": peer * 2 + core}, device_id_type=MESH).start()
        return carry

    lax.fori_loop(1, chips, send_red, 0)
    pltpu.make_async_copy(scale_recv, scale_recv, scale_r).wait()
    pltpu.make_async_copy(recv2, recv2, red_r).wait()

    def add_up(i, sums):
        scale = scale_recv[i]
        return sums + recv2[i].astype(I32).astype(F32) * jnp.concatenate([scale, scale], axis=1)

    total = lax.fori_loop(0, chips, add_up, jnp.zeros((8, columns), F32))
    modes_ref[...] = total
    square = total * total
    power_0 = jnp.sum(square[:, :128], axis=1, keepdims=True)
    power_1 = jnp.sum(square[:, 128:], axis=1, keepdims=True)
    pow_send[...] = jnp.where(iota((8, 128), 1) == 0, power_0, power_1)
    pow_recv[chan] = pow_send[...]
    sends = []
    for i in range(1, nchan):
        peer = lax.rem(chan + i, nchan)
        copy = pltpu.make_async_remote_copy(
            pow_send, pow_recv.at[chan], pow_s.at[i], pow_r.at[i],
            device_id={"chan": peer, "pair": me}, device_id_type=MESH)
        copy.start()
        sends.append(copy)
    for copy in sends:
        copy.wait()
    power = jnp.sum(pow_recv[...], axis=0) * (1.0 / (nchan * sets))
    power_ref[...] = power[:, :2]

    to_core.wait_send()
    pltpu.make_async_copy(meta_send.at[pl.ds(1, n - 1)], meta_send.at[pl.ds(1, n - 1)], meta_s).wait()
    pltpu.make_async_copy(send.at[pl.ds(1, n - 1)], send.at[pl.ds(1, n - 1)], data_s).wait()
    pltpu.make_async_copy(send2.at[pl.ds(1, chips - 1)], send2.at[pl.ds(1, chips - 1)], red_s).wait()
    pltpu.make_async_copy(scale_recv.at[pl.ds(1, chips - 1)], scale_recv.at[pl.ds(1, chips - 1)], scale_s).wait()


def per_device(visibility, pair_counts, owner_ids, slot_ids, beam):
    n, nchan = lax.axis_size("pair"), lax.axis_size("chan")
    rows, columns = visibility.shape[1:]
    mwin, _, base, modes = beam.shape[1:]
    sets = columns // (2 * mwin)
    chips = n // 2
    vmem, hbm = pl.BlockSpec(memory_space=pltpu.VMEM), pl.BlockSpec(memory_space=pl.ANY)
    dma = pltpu.SemaphoreType.DMA
    amplitudes, power = pl.pallas_call(
        functools.partial(body, n, nchan, sets),
        out_shape=(
            jax.ShapeDtypeStruct((8, columns), F32),
            jax.ShapeDtypeStruct((8, mwin), F32),
        ),
        in_specs=[hbm] * 5,
        out_specs=(vmem, vmem),
        scratch_shapes=[
            pltpu.VMEM((1, rows), I32),
            pltpu.VMEM((1, rows), I32),
            pltpu.VMEM((1, rows), I32),
            pltpu.VMEM((rows, columns), BF16),
            pltpu.VMEM((n, 3, 8, 128), BF16),
            pltpu.VMEM((n, 3, 8, 128), BF16),
            pltpu.VMEM((n, 1, 128), F32),
            pltpu.VMEM((n, 1, 128), F32),
            pltpu.VMEM((mwin, 2, base, modes), F32),
            pltpu.VMEM((mwin, 2 * base, modes), BF16),
            pltpu.VMEM((mwin, 2 * base, modes), BF16),
            pltpu.VMEM((base, n * 8), BF16),
            pltpu.VMEM((2 * base, n * 8), BF16),
            pltpu.VMEM((base, 128), F32),
            pltpu.VMEM((chips, 2, 8, columns), F32),
            pltpu.VMEM((chips, 8, columns), F32),
            pltpu.VMEM((chips, 8, columns), I16),
            pltpu.VMEM((chips, 8, columns), I16),
            pltpu.VMEM((1, 128), F32),
            pltpu.VMEM((chips, 1, 128), F32),
            pltpu.VMEM((8, 128), F32),
            pltpu.VMEM((nchan, 8, 128), F32),
            dma((4,)), dma, dma, dma, dma, dma, dma, dma, dma, dma, dma, dma,
            dma((nchan,)), dma((nchan,)),
        ],
        compiler_params=pltpu.CompilerParams(
            collective_id=0, has_side_effects=True
        ),
        name="stack_project",
    )(
        owner_ids.reshape(1, rows), slot_ids.reshape(1, rows), pair_counts.reshape(1, rows),
        visibility[0], beam[0],
    )
    return amplitudes.reshape(1, 8, mwin, 2, sets), power


def solution(mesh):
    in_specs = (
        P("chan", "pair", None),
        P("pair"),
        P("pair", None),
        P("pair"),
        P("chan", None, None, "pair", None),
    )
    out_specs = (P("chan", "pair", None, None, None), P("pair", None))
    return jax.shard_map(
        per_device, mesh=mesh, in_specs=in_specs, out_specs=out_specs, check_vma=False
    )
```

time: 376 us -> 66.9 us (0.18)
  waiting for transfers between devices: 231 us -> 0 us
  local copies, waits for them, and re-layouts: 70.5 us -> 2.69 us
  Pallas kernels: 0 us -> 63.4 us
  starting transfers between devices: 33 us -> 0 us
  between operations: 15 us -> 0.64 us
  other arithmetic: 11 us -> 0 us
  blocking collectives: 8.37 us -> 0 us
    unnamed x2 -> x0, waiting for transfers between devices: 189 us -> none
    pallas_call x0 -> x1, Pallas kernels: none -> 63.4 us  [per_device(): pl.pallas_call(functools.partial(body, n, nchan, sets), out_shape=(jax.Sh...]
    gather x29 -> x0, local copies, waits for them, and re-layouts: 62.5 us -> none  [the longest x10 12.7 us: per_device(): last_at = jnp.searchsorted(sorted_owner, owner_list, side='right')]
    all_to_all x3 -> x0, waiting for transfers between devices: 42.1 us -> none  [the longest x1 28.4 us: per_device(): lax.all_to_all(weighted, 'pair', split_axis=0, concat_axis=0, tiled=True)]
    all_to_all x3 -> x0, starting transfers between devices: 32.7 us -> none  [the longest x1 18.4 us: per_device(): lax.all_to_all(offsets, 'pair', split_axis=0, concat_axis=0, tiled=True)]
    psum x1 -> x0, blocking collectives: 8.37 us -> none  [per_device(): total_power = lax.psum(power_local, 'chan')]
    sort x1 -> x0, other arithmetic: 4.58 us -> none  [per_device(): order = jnp.argsort(owner, stable=True)]
  transfers between devices with their start and end apart: 4 -> 0, of which waited for: 4 -> 0; matrix products, arithmetic and copies ran while one was open for 3% -> 0% of each run, Pallas kernels for 0% -> 0%
where the time goes in v1:
time: 66.9 us; the launch traced here: 66.7 us
  Pallas kernels  63.4 us (95%)
  local copies, waits for them, and re-layouts  2.69 us (4%)
    pallas_call x1, Pallas kernels, per_device(): pl.pallas_call(functools.partial(body, n, nchan, sets), out_shape=(jax.Sh...  63.4 us
    reshape x1, local copies, waits for them, and re-layouts, per_device(): return (amplitudes.reshape(1, 8, mwin, 2, sets), power)  1.38 us

profile of v1, /device:TPU:1, one launch (start us, length us, event | category | flops | bytes accessed | tf_op | source)
XLA Modules:
  0.0 66.7 jit_solution(475816264512886239)
XLA Ops:
  0.6 63.4 %stack_project.1 = (f32[8,256]{1,0:T(8,128)}, f32[8,2]{1,0:T(8,128)}) custom-call(s32[1,512]{1,0:T(1,128)} %bitcast.7, s32[1,512]{1,0:T(1,128)} %bitcast.8, s32[1,512]{1,0:T(1,128)} %bitcast.9, bf16[512,256]{1,0:T(8,128)(2,1)} %bitcast.6, f32[2,2,128,1024]{3,2,1,0:T(8,128)} %bitcast.5), custom_call_target="tpu_custom_call" | custom-call | tf_op jit(solution)/shard_map/stack_project/pallas_call | solution.py:274
  64.0 1.3 %copy.7 = f32[8,2]{0,1:T(2,128)} copy(f32[8,2]{1,0:T(8,128)} %get-tuple-element.7) | data formatting | bytes 128
  65.3 1.4 %reshape.19 = f32[1,8,2,2,64]{4,3,2,1,0:T(2,128)} reshape(f32[8,256]{1,0:T(8,128)} %get-tuple-element.4) | data formatting | bytes 16384 | tf_op jit(solution)/shard_map/reshape | solution.py:316

commit v2 on v1

--- a/solution.py
+++ b/solution.py
@@ -29,7 +29,7 @@
     modes_ref, power_ref,
     owner_ref, slot_ref, count_ref, vis_ref,
     send, recv, meta_send, meta_recv,
-    beam_buf, beam_hi, beam_lo, hot_a, hot_b, inv_denom,
+    beam_buf, beam_t, hot_a, hot_b, bottom, right,
     part, core_recv, send2, recv2, scale_send, scale_recv, pow_send, pow_recv,
     in_sem, beam_sem, meta_s, meta_r, data_s, data_r, core_s, core_r, red_s, red_r, scale_s, scale_r, pow_s, pow_r,
 ):
@@ -53,12 +53,38 @@
 
     barrier = pltpu.get_barrier_semaphore()
 
-    def greet(i, carry):
-        peer = lax.rem(me + i, n)
-        pl.semaphore_signal(barrier, inc=1, device_id={"chan": chan, "pair": peer}, device_id_type=MESH)
-        return carry
-
-    lax.fori_loop(1, n, greet, 0)
+    side = 8
+    while side * side > chips:
+        side //= 2
+    depth = chips // side
+    chip_row, chip_spot = lax.div(chip, side), lax.rem(chip, side)
+
+    def far(k, size):
+        half = lax.div(k, 2) if not isinstance(k, int) else k // 2
+        return size // 2 + half - (k - 2 * half) * (2 * half + 1)
+
+    def each_chip(visit):
+        along = [lax.rem(chip_spot + far(k, side), side) for k in range(side)]
+
+        def ring(k, carry):
+            first = lax.rem(chip_row + far(k, depth), depth) * side
+            for step in along:
+                visit(first + step)
+            return carry
+
+        lax.fori_loop(0, depth - 1, ring, 0)
+        for step in along[:-1]:
+            visit(chip_row * side + step)
+
+    def greet(pair):
+        pl.semaphore_signal(barrier, inc=1, device_id={"chan": chan, "pair": pair}, device_id_type=MESH)
+
+    def greet_chip(peer):
+        greet(peer * 2)
+        greet(peer * 2 + 1)
+
+    each_chip(greet_chip)
+    greet(chip * 2 + 1 - core)
     for i in range(1, nchan):
         peer = lax.rem(chan + i, nchan)
         pl.semaphore_signal(barrier, inc=1, device_id={"chan": peer, "pair": me}, device_id_type=MESH)
@@ -108,38 +134,44 @@
     own_data = pltpu.make_async_copy(send.at[me], recv.at[me], data_r)
     own_data.start()
 
-    def send_meta(i, carry):
-        peer = lax.rem(me + i, n)
+    def ship(peer):
+        target = {"chan": chan, "pair": peer}
         pltpu.make_async_remote_copy(
             meta_send.at[peer], meta_recv.at[me], meta_s, meta_r,
-            device_id={"chan": chan, "pair": peer}, device_id_type=MESH).start()
-        return carry
-
-    lax.fori_loop(1, n, send_meta, 0)
-
-    def send_data(i, carry):
-        peer = lax.rem(me + i, n)
+            device_id=target, device_id_type=MESH).start()
         pltpu.make_async_remote_copy(
             send.at[peer], recv.at[me], data_s, data_r,
-            device_id={"chan": chan, "pair": peer}, device_id_type=MESH).start()
-        return carry
-
-    lax.fori_loop(1, n, send_data, 0)
+            device_id=target, device_id_type=MESH).start()
+
+    def ship_chip(peer):
+        ship(peer * 2 + core)
+        ship(peer * 2 + 1 - core)
+
+    each_chip(ship_chip)
+    ship(chip * 2 + 1 - core)
 
     beam_copy.wait()
     mwin, modes = beam_buf.shape[0], beam_buf.shape[3]
     base = beam_buf.shape[2]
+    width = min(128, modes)
+    turned = width // 2
     for m in range(mwin):
         for r in range(2):
-            def split(i, carry, m=m, r=r):
-                at = pl.ds(i * 16, 16)
-                full = beam_buf[m, r, at, :]
-                high = full.astype(BF16)
-                beam_hi[m, pl.ds(r * base + i * 16, 16), :] = high
-                beam_lo[m, pl.ds(r * base + i * 16, 16), :] = (full - high.astype(F32)).astype(BF16)
+            def turn(i, carry, m=m, r=r):
+                at = pl.ds(pl.multiple_of(i * width, width), width)
+                full = jnp.transpose(beam_buf[m, r, :, at])
+                high = full.astype(BF16).astype(F32)
+                low = full - high
+                high, low = high.reshape(width // 16, 2, 8, base), low.reshape(width // 16, 2, 8, base)
+                to = pl.ds(pl.multiple_of(i * turned, turned), turned)
+                for half in range(2):
+                    beam_t[m, half, to, r * base:(r + 1) * base] = high[:, half].reshape(turned, base).astype(BF16)
+                    beam_t[m, half, to, (2 + r) * base:(3 + r) * base] = low[:, half].reshape(turned, base).astype(BF16)
                 return carry
 
-            lax.fori_loop(0, base // 16, split, 0)
+            lax.fori_loop(0, modes // width, turn, 0)
+
+    right[:, 2 * base:, 128:] = jnp.zeros((mwin, 2 * base, 128), BF16)
 
     pltpu.make_async_copy(meta_recv, meta_recv, meta_r).wait()
     code = jnp.transpose(meta_recv[...].reshape(n, 128))[:16]
@@ -165,50 +197,61 @@
     hot_b[:base] = jnp.where(first, hit_b, 0.0).astype(BF16)
     hot_b[base:] = jnp.where(first, 0.0, hit_b).astype(BF16)
     denom = jnp.sum(hit_a * weight_a + jnp.where(first, hit_b, 0.0) * weight_b, axis=1, keepdims=True)
-    inv_denom[...] = jnp.broadcast_to(jnp.maximum(denom, 1.0), (base, 128))
+    bottom[...] = jnp.broadcast_to(jnp.maximum(denom, 1.0), (base, 128))
 
     pltpu.make_async_copy(recv, recv, data_r).wait()
 
-    rows_0 = recv[:, 0].reshape(n * 8, 128)
-    rows_1 = recv[:, 1].reshape(n * 8, 128)
-    rows_2 = recv[:, 2].reshape(n * 8, 128)
-    late = dot(hot_b[...], rows_2)
-    numer = (dot(hot_a[...], rows_0) + late[:base], dot(hot_a[...], rows_1) + late[base:])
+    early = jnp.concatenate([recv[:, 0].reshape(n * 8, 128), recv[:, 1].reshape(n * 8, 128)], axis=1)
+    numer = dot(hot_a[...], early)
+    late = dot(hot_b[...], recv[:, 2].reshape(n * 8, 128))
+    numer = (numer[:, :128] + late[:base], numer[:, 128:] + late[base:])
     sign = jnp.where(iota((base, 128), 1) < sets, 1.0, -1.0)
     for m in range(mwin):
-        stacked = numer[m] / inv_denom[...]
+        stacked = numer[m] / bottom[...]
         swapped = jnp.concatenate([stacked[:, sets:], stacked[:, :sets]], axis=1) * sign
-        right = jnp.concatenate([jnp.transpose(stacked), jnp.transpose(swapped)], axis=1)
-        high = right.astype(BF16)
-        low = (right - high.astype(F32)).astype(BF16)
-        step_modes = min(256, modes)
-
-        def project(i, carry, m=m, high=high, low=low):
-            at = pl.ds(pl.multiple_of(i * step_modes, step_modes), step_modes)
-            hi = beam_hi[m, :, at]
-            lo = beam_lo[m, :, at]
-            sums = dot(high, hi) + (dot(low, hi) + dot(high, lo))
-            blocks = jnp.transpose(sums).reshape(step_modes // 16, 2, 8, 128)
-            part[pl.ds(i * (step_modes // 16), step_modes // 16), :, :, pl.ds(m * 128, 128)] = blocks
-            return carry
-
-        lax.fori_loop(0, modes // step_modes, project, 0)
-
+        for r, half in enumerate((stacked, swapped)):
+            high = half.astype(BF16)
+            right[m, r * base:(r + 1) * base, :128] = high
+            right[m, (2 + r) * base:(3 + r) * base, :128] = high
+            right[m, r * base:(r + 1) * base, 128:] = (half - high.astype(F32)).astype(BF16)
+
+    step_modes = min(256, modes // 2)
+    step_blocks = step_modes // 8
+
+    def project(parity, to):
+        for m in range(mwin):
+            def step(i, carry, m=m):
+                at = pl.ds(pl.multiple_of(i * step_modes, step_modes), step_modes)
+                both = dot(beam_t[m, parity, at, :], right[m])
+                sums = both[:, :128] + both[:, 128:]
+                part[to, pl.ds(i * step_blocks, step_blocks), :, m * 128:(m + 1) * 128] = sums.reshape(step_blocks, 8, 128)
+                return carry
+
+            lax.fori_loop(0, modes // 2 // step_modes, step, 0)
+
+    project(1 - core, 0)
     to_core = pltpu.make_async_remote_copy(
-        part.at[:, 1 - core], core_recv, core_s, core_r,
-        device_id={"chan": chan, "pair": me + 1 - 2 * core}, device_id_type=MESH)
+        part.at[0], core_recv, core_s, core_r,
+        device_id={"chan": chan, "pair": chip * 2 + 1 - core}, device_id_type=MESH)
     to_core.start()
+    project(core, 1)
     to_core.wait_recv()
-    summed = part[:, core] + core_recv[...]
-    core_recv[...] = summed
-    peak = jnp.max(jnp.abs(summed), axis=(0, 1, 2), keepdims=True).reshape(1, 1)
+
+    def merge(i, top):
+        at = pl.ds(i * step_chips, step_chips)
+        sums = part[1, at] + core_recv[at]
+        part[1, at] = sums
+        return jnp.maximum(top, jnp.max(jnp.abs(sums), axis=0))
+
+    top = lax.fori_loop(0, chips // step_chips, merge, jnp.zeros((8, columns), F32))
+    peak = jnp.max(jnp.max(top, axis=1, keepdims=True), axis=0, keepdims=True)
     peak = jnp.maximum(peak, 1e-30)
     scale_send[...] = jnp.broadcast_to(peak * (1.0 / 32000.0), (1, 128))
     factor = jnp.broadcast_to(32000.0 / peak, (8, columns))
 
     def code_sums(i, carry):
-        scaled = core_recv[pl.ds(i * step_chips, step_chips)] * factor
-        send2[pl.ds(i * step_chips, step_chips)] = jnp.round(scaled).astype(I32).astype(I16)
+        at = pl.ds(i * step_chips, step_chips)
+        send2[at] = jnp.round(part[1, at] * factor).astype(I32).astype(I16)
         return carry
 
     lax.fori_loop(0, chips // step_chips, code_sums, 0)
@@ -218,25 +261,26 @@
     own_red = pltpu.make_async_copy(send2.at[chip], recv2.at[chip], red_r)
     own_red.start()
 
-    def send_red(i, carry):
-        peer = lax.rem(chip + i, chips)
+    def send_red(peer):
+        target = {"chan": chan, "pair": peer * 2 + core}
         pltpu.make_async_remote_copy(
-            scale_send, scale_recv.at[chip], scale_s, scale_r,
-            device_id={"chan": chan, "pair": peer * 2 + core}, device_id_type=MESH).start()
+            send2.at[peer], recv2.at[chip], red_s, red_r, device_id=target, device_id_type=MESH).start()
         pltpu.make_async_remote_copy(
-            send2.at[peer], recv2.at[chip], red_s, red_r,
-            device_id={"chan": chan, "pair": peer * 2 + core}, device_id_type=MESH).start()
-        return carry
-
-    lax.fori_loop(1, chips, send_red, 0)
+            scale_send, scale_recv.at[chip], scale_s, scale_r, device_id=target, device_id_type=MESH).start()
+
+    each_chip(send_red)
     pltpu.make_async_copy(scale_recv, scale_recv, scale_r).wait()
     pltpu.make_async_copy(recv2, recv2, red_r).wait()
 
+    step_adds = min(8, chips)
+
     def add_up(i, sums):
-        scale = scale_recv[i]
-        return sums + recv2[i].astype(I32).astype(F32) * jnp.concatenate([scale, scale], axis=1)
-
-    total = lax.fori_loop(0, chips, add_up, jnp.zeros((8, columns), F32))
+        for j in range(step_adds):
+            scale = scale_recv[i * step_adds + j]
+            sums = sums + recv2[i * step_adds + j].astype(I32).astype(F32) * jnp.concatenate([scale, scale], axis=1)
+        return sums
+
+    total = lax.fori_loop(0, chips // step_adds, add_up, jnp.zeros((8, columns), F32))
     modes_ref[...] = total
     square = total * total
     power_0 = jnp.sum(square[:, :128], axis=1, keepdims=True)
@@ -269,7 +313,7 @@
     mwin, _, base, modes = beam.shape[1:]
     sets = columns // (2 * mwin)
     chips = n // 2
-    vmem, hbm = pl.BlockSpec(memory_space=pltpu.VMEM), pl.BlockSpec(memory_space=pl.ANY)
+    vmem, hbm = pl.BlockSpec(memory_space=pltpu.VMEM), pl.BlockSpec(memory_space=pltpu.HBM)
     dma = pltpu.SemaphoreType.DMA
     amplitudes, power = pl.pallas_call(
         functools.partial(body, n, nchan, sets),
@@ -289,12 +333,12 @@
             pltpu.VMEM((n, 1, 128), F32),
             pltpu.VMEM((n, 1, 128), F32),
             pltpu.VMEM((mwin, 2, base, modes), F32),
-            pltpu.VMEM((mwin, 2 * base, modes), BF16),
-            pltpu.VMEM((mwin, 2 * base, modes), BF16),
+            pltpu.VMEM((mwin, 2, modes // 2, 4 * base), BF16),
             pltpu.VMEM((base, n * 8), BF16),
             pltpu.VMEM((2 * base, n * 8), BF16),
             pltpu.VMEM((base, 128), F32),
-            pltpu.VMEM((chips, 2, 8, columns), F32),
+            pltpu.VMEM((mwin, 4 * base, 256), BF16),
+            pltpu.VMEM((2, chips, 8, columns), F32),
             pltpu.VMEM((chips, 8, columns), F32),
             pltpu.VMEM((chips, 8, columns), I16),
             pltpu.VMEM((chips, 8, columns), I16),

time: 66.9 us -> 63 us (0.942)
  Pallas kernels: 63.4 us -> 59.5 us
    pallas_call x1, Pallas kernels: 63.4 us -> 59.5 us  [per_device(): pl.pallas_call(functools.partial(body, n, nchan, sets), out_shape=(jax.Sh...]
where the time goes in v2:
time: 63 us; the launch traced here: 62.8 us
  Pallas kernels  59.5 us (94%)
  local copies, waits for them, and re-layouts  2.69 us (4%)
  between operations  0.64 us (1%)
    pallas_call x1, Pallas kernels, per_device(): pl.pallas_call(functools.partial(body, n, nchan, sets), out_shape=(jax.Sh...  59.5 us
    reshape x1, local copies, waits for them, and re-layouts, per_device(): return (amplitudes.reshape(1, 8, mwin, 2, sets), power)  1.38 us
    unnamed x1, local copies, waits for them, and re-layouts  1.31 us

profile of v2, /device:TPU:1, one launch (start us, length us, event | category | flops | bytes accessed | tf_op | source)
XLA Modules:
  0.0 62.8 jit_solution(12040385879501120422)
XLA Ops:
  0.6 59.5 %stack_project.1 = (f32[8,256]{1,0:T(8,128)}, f32[8,2]{1,0:T(8,128)}) custom-call(s32[1,512]{1,0:T(1,128)} %bitcast.7, s32[1,512]{1,0:T(1,128)} %bitcast.8, s32[1,512]{1,0:T(1,128)} %bitcast.9, bf16[512,256]{1,0:T(8,128)(2,1)} %bitcast.6, f32[2,2,128,1024]{3,2,1,0:T(8,128)} %bitcast.5), custom_call_target="tpu_custom_call" | custom-call | tf_op jit(solution)/shard_map/stack_project/pallas_call | solution.py:318
  60.1 1.3 %copy.7 = f32[8,2]{0,1:T(2,128)} copy(f32[8,2]{1,0:T(8,128)} %get-tuple-element.7) | data formatting | bytes 128
  61.4 1.4 %reshape.19 = f32[1,8,2,2,64]{4,3,2,1,0:T(2,128)} reshape(f32[8,256]{1,0:T(8,128)} %get-tuple-element.4) | data formatting | bytes 16384 | tf_op jit(solution)/shard_map/reshape | solution.py:360

commit v3 on v2

--- a/solution.py
+++ b/solution.py
@@ -26,12 +26,12 @@
 def body(
     n, nchan, sets,
     owner_hbm, slot_hbm, count_hbm, vis_hbm, beam_hbm,
-    modes_ref, power_ref,
+    result_ref,
     owner_ref, slot_ref, count_ref, vis_ref,
     send, recv, meta_send, meta_recv,
     beam_buf, beam_t, hot_a, hot_b, bottom, right,
     part, core_recv, send2, recv2, scale_send, scale_recv, pow_send, pow_recv,
-    in_sem, beam_sem, meta_s, meta_r, data_s, data_r, core_s, core_r, red_s, red_r, scale_s, scale_r, pow_s, pow_r,
+    in_sem, beam_sem, meta_s, meta_r, hand_s, hand_r, data_s, data_r, core_s, core_r, red_s, red_r, scale_s, scale_r, pow_s, pow_r,
 ):
     chan = lax.axis_index("chan")
     me = lax.axis_index("pair")
@@ -72,9 +72,9 @@
                 visit(first + step)
             return carry
 
-        lax.fori_loop(0, depth - 1, ring, 0)
         for step in along[:-1]:
             visit(chip_row * side + step)
+        lax.fori_loop(0, depth - 1, ring, 0)
 
     def greet(pair):
         pl.semaphore_signal(barrier, inc=1, device_id={"chan": chan, "pair": pair}, device_id_type=MESH)
@@ -129,19 +129,40 @@
 
     pl.semaphore_wait(barrier, n - 1 + nchan - 1)
 
-    own_meta = pltpu.make_async_copy(meta_send.at[me], meta_recv.at[me], meta_r)
-    own_meta.start()
+    def send_meta(pair):
+        pltpu.make_async_remote_copy(
+            meta_send.at[pair], meta_recv.at[me], meta_s, meta_r,
+            device_id={"chan": chan, "pair": pair}, device_id_type=MESH).start()
+
+    groups = chips // nchan
+    group = lax.div(chip, nchan)
+    keeper = lax.rem(chip, nchan) == chan
+
+    def send_metas(i, carry):
+        peer = lax.rem(group + i, groups) * nchan + chan
+        send_meta(peer * 2)
+        send_meta(peer * 2 + 1)
+        return carry
+
+    lax.fori_loop(1, groups, send_metas, 0)
+
+    @pl.when(keeper)
+    def _():
+        send_meta(chip * 2 + 1 - core)
+        pltpu.make_async_copy(meta_send.at[me], meta_recv.at[me], meta_r).start()
+
+    @pl.when(jnp.logical_not(keeper))
+    def _():
+        send_meta((group * nchan + chan) * 2)
+        send_meta((group * nchan + chan) * 2 + 1)
+
     own_data = pltpu.make_async_copy(send.at[me], recv.at[me], data_r)
     own_data.start()
 
     def ship(peer):
-        target = {"chan": chan, "pair": peer}
-        pltpu.make_async_remote_copy(
-            meta_send.at[peer], meta_recv.at[me], meta_s, meta_r,
-            device_id=target, device_id_type=MESH).start()
         pltpu.make_async_remote_copy(
             send.at[peer], recv.at[me], data_s, data_r,
-            device_id=target, device_id_type=MESH).start()
+            device_id={"chan": chan, "pair": peer}, device_id_type=MESH).start()
 
     def ship_chip(peer):
         ship(peer * 2 + core)
@@ -173,7 +194,18 @@
 
     right[:, 2 * base:, 128:] = jnp.zeros((mwin, 2 * base, 128), BF16)
 
-    pltpu.make_async_copy(meta_recv, meta_recv, meta_r).wait()
+    @pl.when(keeper)
+    def _():
+        pltpu.make_async_copy(meta_recv, meta_recv, meta_r).wait()
+        for i in range(1, nchan):
+            pltpu.make_async_remote_copy(
+                meta_recv, meta_recv, hand_s.at[i], hand_r,
+                device_id={"chan": lax.rem(chan + i, nchan), "pair": me}, device_id_type=MESH).start()
+
+    @pl.when(jnp.logical_not(keeper))
+    def _():
+        pltpu.make_async_copy(meta_recv, meta_recv, hand_r).wait()
+
     code = jnp.transpose(meta_recv[...].reshape(n, 128))[:16]
     weight = jnp.floor(code * (1.0 / 128.0))
     place = code - weight * 128.0
@@ -218,40 +250,46 @@
     step_modes = min(256, modes // 2)
     step_blocks = step_modes // 8
 
-    def project(parity, to):
-        for m in range(mwin):
-            def step(i, carry, m=m):
-                at = pl.ds(pl.multiple_of(i * step_modes, step_modes), step_modes)
-                both = dot(beam_t[m, parity, at, :], right[m])
-                sums = both[:, :128] + both[:, 128:]
-                part[to, pl.ds(i * step_blocks, step_blocks), :, m * 128:(m + 1) * 128] = sums.reshape(step_blocks, 8, 128)
-                return carry
-
-            lax.fori_loop(0, modes // 2 // step_modes, step, 0)
-
-    project(1 - core, 0)
-    to_core = pltpu.make_async_remote_copy(
-        part.at[0], core_recv, core_s, core_r,
-        device_id={"chan": chan, "pair": chip * 2 + 1 - core}, device_id_type=MESH)
-    to_core.start()
-    project(core, 1)
-    to_core.wait_recv()
+    def project(parity, to, m):
+        def step(i, carry):
+            at = pl.ds(pl.multiple_of(i * step_modes, step_modes), step_modes)
+            both = dot(beam_t[m, parity, at, :], right[m])
+            sums = both[:, :128] + both[:, 128:]
+            part[to, m, pl.ds(i * step_blocks, step_blocks)] = sums.reshape(step_blocks, 8, 128)
+            return carry
+
+        lax.fori_loop(0, modes // 2 // step_modes, step, 0)
+
+    to_core = []
+    for m in range(mwin):
+        project(1 - core, 0, m)
+        to_core.append(pltpu.make_async_remote_copy(
+            part.at[0, m], core_recv.at[m], core_s.at[m], core_r.at[m],
+            device_id={"chan": chan, "pair": chip * 2 + 1 - core}, device_id_type=MESH))
+        to_core[m].start()
+    for m in range(mwin):
+        project(core, 1, m)
+    for m in range(mwin):
+        to_core[m].wait_recv()
 
     def merge(i, top):
         at = pl.ds(i * step_chips, step_chips)
-        sums = part[1, at] + core_recv[at]
-        part[1, at] = sums
-        return jnp.maximum(top, jnp.max(jnp.abs(sums), axis=0))
-
-    top = lax.fori_loop(0, chips // step_chips, merge, jnp.zeros((8, columns), F32))
+        for m in range(mwin):
+            sums = part[1, m, at] + core_recv[m, at]
+            part[1, m, at] = sums
+            top = jnp.maximum(top, jnp.max(jnp.abs(sums), axis=0))
+        return top
+
+    top = lax.fori_loop(0, chips // step_chips, merge, jnp.zeros((8, 128), F32))
     peak = jnp.max(jnp.max(top, axis=1, keepdims=True), axis=0, keepdims=True)
     peak = jnp.maximum(peak, 1e-30)
     scale_send[...] = jnp.broadcast_to(peak * (1.0 / 32000.0), (1, 128))
-    factor = jnp.broadcast_to(32000.0 / peak, (8, columns))
+    factor = jnp.broadcast_to(32000.0 / peak, (8, 128))
 
     def code_sums(i, carry):
         at = pl.ds(i * step_chips, step_chips)
-        send2[at] = jnp.round(part[1, at] * factor).astype(I32).astype(I16)
+        scaled = jnp.concatenate([part[1, 0, at] * factor, part[1, 1, at] * factor], axis=2)
+        send2[at] = jnp.round(scaled).astype(I32).astype(I16)
         return carry
 
     lax.fori_loop(0, chips // step_chips, code_sums, 0)
@@ -281,7 +319,7 @@
         return sums
 
     total = lax.fori_loop(0, chips // step_adds, add_up, jnp.zeros((8, columns), F32))
-    modes_ref[...] = total
+    result_ref[:, :columns] = total
     square = total * total
     power_0 = jnp.sum(square[:, :128], axis=1, keepdims=True)
     power_1 = jnp.sum(square[:, 128:], axis=1, keepdims=True)
@@ -298,13 +336,33 @@
     for copy in sends:
         copy.wait()
     power = jnp.sum(pow_recv[...], axis=0) * (1.0 / (nchan * sets))
-    power_ref[...] = power[:, :2]
-
-    to_core.wait_send()
-    pltpu.make_async_copy(meta_send.at[pl.ds(1, n - 1)], meta_send.at[pl.ds(1, n - 1)], meta_s).wait()
+    result_ref[:, columns:] = power
+
+    for copy in to_core:
+        copy.wait_send()
+    sent = 2 * groups
+
+    @pl.when(keeper)
+    def _():
+        pltpu.make_async_copy(meta_send.at[pl.ds(0, sent - 1)], meta_send.at[pl.ds(0, sent - 1)], meta_s).wait()
+        for i in range(1, nchan):
+            pltpu.make_async_copy(meta_recv, meta_recv, hand_s.at[i]).wait()
+
+    @pl.when(jnp.logical_not(keeper))
+    def _():
+        pltpu.make_async_copy(meta_send.at[pl.ds(0, sent)], meta_send.at[pl.ds(0, sent)], meta_s).wait()
+
     pltpu.make_async_copy(send.at[pl.ds(1, n - 1)], send.at[pl.ds(1, n - 1)], data_s).wait()
     pltpu.make_async_copy(send2.at[pl.ds(1, chips - 1)], send2.at[pl.ds(1, chips - 1)], red_s).wait()
     pltpu.make_async_copy(scale_recv.at[pl.ds(1, chips - 1)], scale_recv.at[pl.ds(1, chips - 1)], scale_s).wait()
+
+
+def shape_results(mwin, sets, result_ref, modes_ref, power_ref):
+    for m in range(mwin):
+        for part in range(2):
+            at = (2 * m + part) * sets
+            modes_ref[:, m, part, :] = result_ref[:, at:at + sets]
+    power_ref[...] = jnp.transpose(result_ref[:, 2 * mwin * sets:])[:mwin]
 
 
 def per_device(visibility, pair_counts, owner_ids, slot_ids, beam):
@@ -315,14 +373,11 @@
     chips = n // 2
     vmem, hbm = pl.BlockSpec(memory_space=pltpu.VMEM), pl.BlockSpec(memory_space=pltpu.HBM)
     dma = pltpu.SemaphoreType.DMA
-    amplitudes, power = pl.pallas_call(
+    result = pl.pallas_call(
         functools.partial(body, n, nchan, sets),
-        out_shape=(
-            jax.ShapeDtypeStruct((8, columns), F32),
-            jax.ShapeDtypeStruct((8, mwin), F32),
-        ),
+        out_shape=jax.ShapeDtypeStruct((8, columns + 128), F32),
         in_specs=[hbm] * 5,
-        out_specs=(vmem, vmem),
+        out_specs=vmem,
         scratch_shapes=[
             pltpu.VMEM((1, rows), I32),
             pltpu.VMEM((1, rows), I32),
@@ -338,15 +393,15 @@
             pltpu.VMEM((2 * base, n * 8), BF16),
             pltpu.VMEM((base, 128), F32),
             pltpu.VMEM((mwin, 4 * base, 256), BF16),
-            pltpu.VMEM((2, chips, 8, columns), F32),
-            pltpu.VMEM((chips, 8, columns), F32),
+            pltpu.VMEM((2, mwin, chips, 8, 128), F32),
+            pltpu.VMEM((mwin, chips, 8, 128), F32),
             pltpu.VMEM((chips, 8, columns), I16),
             pltpu.VMEM((chips, 8, columns), I16),
             pltpu.VMEM((1, 128), F32),
             pltpu.VMEM((chips, 1, 128), F32),
             pltpu.VMEM((8, 128), F32),
             pltpu.VMEM((nchan, 8, 128), F32),
-            dma((4,)), dma, dma, dma, dma, dma, dma, dma, dma, dma, dma, dma,
+            dma((4,)), dma, dma, dma, dma((nchan,)), dma, dma, dma, dma((mwin,)), dma((mwin,)), dma, dma, dma, dma,
             dma((nchan,)), dma((nchan,)),
         ],
         compiler_params=pltpu.CompilerParams(
@@ -357,7 +412,14 @@
         owner_ids.reshape(1, rows), slot_ids.reshape(1, rows), pair_counts.reshape(1, rows),
         visibility[0], beam[0],
     )
-    return amplitudes.reshape(1, 8, mwin, 2, sets), power
+    shaped, power = pl.pallas_call(
+        functools.partial(shape_results, mwin, sets),
+        out_shape=(jax.ShapeDtypeStruct((8, mwin, 2, sets), F32), jax.ShapeDtypeStruct((mwin, 8), F32)),
+        in_specs=[vmem],
+        out_specs=(vmem, vmem),
+        name="shape_results",
+    )(result)
+    return shaped[None], power.T
 
 
 def solution(mesh):

time: 63 us -> 60.3 us (0.957)
  local copies, waits for them, and re-layouts: 2.69 us -> 0 us
    reshape x1 -> x0, local copies, waits for them, and re-layouts: 1.38 us -> none  [per_device(): return (amplitudes.reshape(1, 8, mwin, 2, sets), power)]
    unnamed x1 -> x0, local copies, waits for them, and re-layouts: 1.31 us -> none
    pallas_call x1 -> x2, Pallas kernels: 59.5 us -> 59.4 us  [the longest x1 58 us: per_device(): pl.pallas_call(functools.partial(body, n, nchan, sets), out_shape=jax.Sha...]
where the time goes in v3:
time: 60.3 us; the launch traced here: 60 us
  Pallas kernels  59.4 us (99%)
  between operations  0.64 us (1%)
    pallas_call x1, Pallas kernels, per_device(): pl.pallas_call(functools.partial(body, n, nchan, sets), out_shape=jax.Sha...  58 us
    pallas_call x1, Pallas kernels, per_device(): pl.pallas_call(functools.partial(shape_results, mwin, sets), out_shape=(j...  1.41 us

profile of v3, /device:TPU:1, one launch (start us, length us, event | category | flops | bytes accessed | tf_op | source)
XLA Modules:
  0.0 60.0 jit_solution(14988459140593360318)
XLA Ops:
  0.6 58.0 %stack_project.1.result_ref = f32[8,384]{1,0:T(8,128)} custom-call(s32[1,512]{1,0:T(1,128)} %bitcast.9, s32[1,512]{1,0:T(1,128)} %bitcast.10, s32[1,512]{1,0:T(1,128)} %bitcast.11, bf16[512,256]{1,0:T(8,128)(2,1)} %bitcast.8, f32[2,2,128,1024]{3,2,1,0:T(8,128)} %bitcast.7), custom_call_target="tpu_custom_call" | custom-call | tf_op jit(solution)/shard_map/stack_project/pallas_call | solution.py:376
  58.6 1.4 %shape_results.1 = (f32[8,2,2,64]{3,2,1,0:T(2,128)}, f32[2,8]{1,0:T(2,128)}) custom-call(f32[8,384]{1,0:T(8,128)} %stack_project.1.result_ref), custom_call_target="tpu_custom_call" | custom-call | tf_op jit(solution)/shard_map/shape_results/pallas_call | solution.py:415

commit v4 on v3

--- a/solution.py
+++ b/solution.py
@@ -21,6 +21,13 @@
 
 def dot_nt(a, b):
     return lax.dot_general(a, b, (((1,), (1,)), ((), ())), preferred_element_type=F32)
+
+
+def ring_size(chips):
+    side = 8
+    while side * side > chips:
+        side //= 2
+    return side
 
 
 def body(
@@ -31,7 +38,7 @@
     send, recv, meta_send, meta_recv,
     beam_buf, beam_t, hot_a, hot_b, bottom, right,
     part, core_recv, send2, recv2, scale_send, scale_recv, pow_send, pow_recv,
-    in_sem, beam_sem, meta_s, meta_r, hand_s, hand_r, data_s, data_r, core_s, core_r, red_s, red_r, scale_s, scale_r, pow_s, pow_r,
+    hellos, in_sem, beam_sem, meta_s, meta_r, hand_s, hand_r, data_s, data_r, core_s, core_r, red_s, red_r, scale_s, scale_r, pow_s, pow_r,
 ):
     chan = lax.axis_index("chan")
     me = lax.axis_index("pair")
@@ -53,9 +60,7 @@
 
     barrier = pltpu.get_barrier_semaphore()
 
-    side = 8
-    while side * side > chips:
-        side //= 2
+    side = ring_size(chips)
     depth = chips // side
     chip_row, chip_spot = lax.div(chip, side), lax.rem(chip, side)
 
@@ -76,18 +81,56 @@
             visit(chip_row * side + step)
         lax.fori_loop(0, depth - 1, ring, 0)
 
-    def greet(pair):
-        pl.semaphore_signal(barrier, inc=1, device_id={"chan": chan, "pair": pair}, device_id_type=MESH)
-
-    def greet_chip(peer):
-        greet(peer * 2)
-        greet(peer * 2 + 1)
-
-    each_chip(greet_chip)
-    greet(chip * 2 + 1 - core)
+    group_size = depth * 2
+    my_place = chip_row * 2 + core
+
+    def pair_at(spot, line, which):
+        return (line * side + spot) * 2 + which
+
+    def greet(sem, pair):
+        pl.semaphore_signal(sem, inc=1, device_id={"chan": chan, "pair": pair}, device_id_type=MESH)
+
+    def greet_group(sem, spot):
+        for line in range(depth):
+            for which in range(2):
+                greet(sem, pair_at(spot, line, which))
+
+    def greet_later(spot, carry):
+        greet_group(barrier, spot)
+        return carry
+
+    def greet_own(sem):
+        def line_of(line, carry):
+            greet(sem, pair_at(chip_spot, line, 0))
+            greet(sem, pair_at(chip_spot, line, 1))
+            return carry
+        return line_of
+
+    @pl.when(core == 0)
+    def _():
+        greet(barrier, me + 1)
+
+    lax.fori_loop(chip_row + 1, depth, greet_own(barrier), 0)
     for i in range(1, nchan):
         peer = lax.rem(chan + i, nchan)
         pl.semaphore_signal(barrier, inc=1, device_id={"chan": peer, "pair": me}, device_id_type=MESH)
+    lax.fori_loop(chip_spot + 1, side, greet_later, 0)
+
+    pl.semaphore_wait(barrier, chip_spot * group_size + my_place + nchan - 1)
+
+    hello = hellos.at[chip_spot]
+
+    @pl.when(core == 1)
+    def _():
+        greet(hello, me - 1)
+
+    lax.fori_loop(0, chip_row, greet_own(hello), 0)
+
+    def greet_earlier(i, carry):
+        greet_group(hello, chip_spot - i)
+        return carry
+
+    lax.fori_loop(1, chip_spot + 1, greet_earlier, 0)
 
     for load in loads:
         load.wait()
@@ -127,49 +170,57 @@
 
     lax.fori_loop(0, n // step_owners, pack, 0)
 
-    pl.semaphore_wait(barrier, n - 1 + nchan - 1)
-
-    def send_meta(pair):
+    keeper = lax.rem(chip_spot, nchan) == chan
+
+    def ship(pair):
+        pltpu.make_async_remote_copy(
+            send.at[pair], recv.at[me], data_s, data_r,
+            device_id={"chan": chan, "pair": pair}, device_id_type=MESH).start()
+
+    def ship_meta(pair):
         pltpu.make_async_remote_copy(
             meta_send.at[pair], meta_recv.at[me], meta_s, meta_r,
             device_id={"chan": chan, "pair": pair}, device_id_type=MESH).start()
 
-    groups = chips // nchan
-    group = lax.div(chip, nchan)
-    keeper = lax.rem(chip, nchan) == chan
-
-    def send_metas(i, carry):
-        peer = lax.rem(group + i, groups) * nchan + chan
-        send_meta(peer * 2)
-        send_meta(peer * 2 + 1)
-        return carry
-
-    lax.fori_loop(1, groups, send_metas, 0)
+    lines = [lax.rem(chip_row + far(k, depth), depth) for k in range(depth)]
+
+    def ship_group(spot, own):
+        def every(visit):
+            for line in lines[:depth - 1 if own else depth]:
+                visit(pair_at(spot, line, core))
+                visit(pair_at(spot, line, 1 - core))
+            if own:
+                visit(chip * 2 + 1 - core)
+
+        @pl.when(lax.rem(spot, nchan) == chan)
+        def _():
+            every(ship_meta)
+
+        every(ship)
+
+    def ship_earlier(i, carry):
+        ship_group(chip_spot - i, False)
+        return carry
+
+    def ship_later(spot, carry):
+        pl.semaphore_wait(hellos.at[spot], group_size)
+        ship_group(spot, False)
+        return carry
 
     @pl.when(keeper)
     def _():
-        send_meta(chip * 2 + 1 - core)
         pltpu.make_async_copy(meta_send.at[me], meta_recv.at[me], meta_r).start()
-
-    @pl.when(jnp.logical_not(keeper))
-    def _():
-        send_meta((group * nchan + chan) * 2)
-        send_meta((group * nchan + chan) * 2 + 1)
 
     own_data = pltpu.make_async_copy(send.at[me], recv.at[me], data_r)
     own_data.start()
-
-    def ship(peer):
-        pltpu.make_async_remote_copy(
-            send.at[peer], recv.at[me], data_s, data_r,
-            device_id={"chan": chan, "pair": peer}, device_id_type=MESH).start()
-
-    def ship_chip(peer):
-        ship(peer * 2 + core)
-        ship(peer * 2 + 1 - core)
-
-    each_chip(ship_chip)
-    ship(chip * 2 + 1 - core)
+    lax.fori_loop(1, chip_spot + 1, ship_earlier, 0)
+
+    @pl.when(my_place < group_size - 1)
+    def _():
+        pl.semaphore_wait(hello, group_size - 1 - my_place)
+
+    ship_group(chip_spot, True)
+    lax.fori_loop(chip_spot + 1, side, ship_later, 0)
 
     beam_copy.wait()
     mwin, modes = beam_buf.shape[0], beam_buf.shape[3]
@@ -340,7 +391,7 @@
 
     for copy in to_core:
         copy.wait_send()
-    sent = 2 * groups
+    sent = group_size * (side // nchan)
 
     @pl.when(keeper)
     def _():
@@ -401,7 +452,7 @@
             pltpu.VMEM((chips, 1, 128), F32),
             pltpu.VMEM((8, 128), F32),
             pltpu.VMEM((nchan, 8, 128), F32),
-            dma((4,)), dma, dma, dma, dma((nchan,)), dma, dma, dma, dma((mwin,)), dma((mwin,)), dma, dma, dma, dma,
+            pltpu.SemaphoreType.REGULAR((ring_size(n // 2),)), dma((4,)), dma, dma, dma, dma((nchan,)), dma, dma, dma, dma((mwin,)), dma((mwin,)), dma, dma, dma, dma,
             dma((nchan,)), dma((nchan,)),
         ],
         compiler_params=pltpu.CompilerParams(

time: 60.3 us -> 74.6 us (1.24)
  Pallas kernels: 59.4 us -> 73.5 us
    pallas_call x1, Pallas kernels: 58 us -> 72.1 us  [per_device(): pl.pallas_call(functools.partial(body, n, nchan, sets), out_shape=jax.Sha...]
where the time goes in v4:
time: 74.6 us; the launch traced here: 74.1 us
  Pallas kernels  73.5 us (99%)
    pallas_call x1, Pallas kernels, per_device(): pl.pallas_call(functools.partial(body, n, nchan, sets), out_shape=jax.Sha...  72.1 us

profile of v4, /device:TPU:1, one launch (start us, length us, event | category | flops | bytes accessed | tf_op | source)
XLA Modules:
  0.0 74.1 jit_solution(9396066599007344222)
XLA Ops:
  0.6 72.1 %stack_project.1.result_ref = f32[8,384]{1,0:T(8,128)} custom-call(s32[1,512]{1,0:T(1,128)} %bitcast.9, s32[1,512]{1,0:T(1,128)} %bitcast.10, s32[1,512]{1,0:T(1,128)} %bitcast.11, bf16[512,256]{1,0:T(8,128)(2,1)} %bitcast.8, f32[2,2,128,1024]{3,2,1,0:T(8,128)} %bitcast.7), custom_call_target="tpu_custom_call" | custom-call | tf_op jit(solution)/shard_map/stack_project/pallas_call | solution.py:427
  72.7 1.4 %shape_results.1 = (f32[8,2,2,64]{3,2,1,0:T(2,128)}, f32[2,8]{1,0:T(2,128)}) custom-call(f32[8,384]{1,0:T(8,128)} %stack_project.1.result_ref), custom_call_target="tpu_custom_call" | custom-call | tf_op jit(solution)/shard_map/shape_results/pallas_call | solution.py:466

commit v5 on v3

--- a/solution.py
+++ b/solution.py
@@ -26,12 +26,12 @@
 def body(
     n, nchan, sets,
     owner_hbm, slot_hbm, count_hbm, vis_hbm, beam_hbm,
-    result_ref,
+    result_hbm, power_hbm,
     owner_ref, slot_ref, count_ref, vis_ref,
     send, recv, meta_send, meta_recv,
     beam_buf, beam_t, hot_a, hot_b, bottom, right,
-    part, core_recv, send2, recv2, scale_send, scale_recv, pow_send, pow_recv,
-    in_sem, beam_sem, meta_s, meta_r, hand_s, hand_r, data_s, data_r, core_s, core_r, red_s, red_r, scale_s, scale_r, pow_s, pow_r,
+    part, core_recv, send2, recv2, scale_send, scale_recv, total_buf, pow_send,
+    in_sem, beam_sem, meta_s, meta_r, hand_s, hand_r, data_s, data_r, core_s, core_r, red_s, red_r, scale_s, scale_r, pow_s, pow_r, out_sem, own_sem,
 ):
     chan = lax.axis_index("chan")
     me = lax.axis_index("pair")
@@ -64,17 +64,18 @@
         return size // 2 + half - (k - 2 * half) * (2 * half + 1)
 
     def each_chip(visit):
-        along = [lax.rem(chip_spot + far(k, side), side) for k in range(side)]
-
-        def ring(k, carry):
-            first = lax.rem(chip_row + far(k, depth), depth) * side
-            for step in along:
-                visit(first + step)
-            return carry
-
-        for step in along[:-1]:
-            visit(chip_row * side + step)
-        lax.fori_loop(0, depth - 1, ring, 0)
+        for k in range(side - 1):
+            visit(chip_row * side + lax.rem(chip_spot + far(k, side), side))
+
+        def diagonal(total, carry):
+            def step(k, carry):
+                line = lax.rem(chip_row + far(k, depth), depth)
+                visit(line * side + lax.rem(chip_spot + far(total - k, side), side))
+                return carry
+
+            return lax.fori_loop(lax.max(0, total - side + 1), lax.min(depth - 1, total + 1), step, carry)
+
+        lax.fori_loop(0, depth + side - 2, diagonal, 0)
 
     def greet(pair):
         pl.semaphore_signal(barrier, inc=1, device_id={"chan": chan, "pair": pair}, device_id_type=MESH)
@@ -250,37 +251,39 @@
     step_modes = min(256, modes // 2)
     step_blocks = step_modes // 8
 
-    def project(parity, to, m):
-        def step(i, carry):
-            at = pl.ds(pl.multiple_of(i * step_modes, step_modes), step_modes)
-            both = dot(beam_t[m, parity, at, :], right[m])
-            sums = both[:, :128] + both[:, 128:]
-            part[to, m, pl.ds(i * step_blocks, step_blocks)] = sums.reshape(step_blocks, 8, 128)
-            return carry
-
-        lax.fori_loop(0, modes // 2 // step_modes, step, 0)
+    pieces = modes // 2 // step_modes
+
+    def project(parity, to, m, i):
+        both = dot(beam_t[m, parity, i * step_modes:(i + 1) * step_modes, :], right[m])
+        sums = both[:, :128] + both[:, 128:]
+        part[to, m, i * step_blocks:(i + 1) * step_blocks] = sums.reshape(step_blocks, 8, 128)
 
     to_core = []
     for m in range(mwin):
-        project(1 - core, 0, m)
-        to_core.append(pltpu.make_async_remote_copy(
-            part.at[0, m], core_recv.at[m], core_s.at[m], core_r.at[m],
-            device_id={"chan": chan, "pair": chip * 2 + 1 - core}, device_id_type=MESH))
-        to_core[m].start()
-    for m in range(mwin):
-        project(core, 1, m)
-    for m in range(mwin):
-        to_core[m].wait_recv()
-
-    def merge(i, top):
-        at = pl.ds(i * step_chips, step_chips)
-        for m in range(mwin):
-            sums = part[1, m, at] + core_recv[m, at]
-            part[1, m, at] = sums
-            top = jnp.maximum(top, jnp.max(jnp.abs(sums), axis=0))
-        return top
-
-    top = lax.fori_loop(0, chips // step_chips, merge, jnp.zeros((8, 128), F32))
+        for i in range(pieces):
+            project(1 - core, 0, m, i)
+            at = pl.ds(i * step_blocks, step_blocks)
+            to_core.append(pltpu.make_async_remote_copy(
+                part.at[0, m, at], core_recv.at[m, at], core_s.at[m, i], core_r.at[m, i],
+                device_id={"chan": chan, "pair": chip * 2 + 1 - core}, device_id_type=MESH))
+            to_core[-1].start()
+    for m in range(mwin):
+        for i in range(pieces):
+            project(core, 1, m, i)
+
+    top = jnp.zeros((8, 128), F32)
+    step_chips = min(8, step_blocks)
+    for m in range(mwin):
+        for i in range(pieces):
+            to_core[m * pieces + i].wait_recv()
+
+            def merge(j, top, m=m, i=i):
+                at = pl.ds(i * step_blocks + j * step_chips, step_chips)
+                sums = part[1, m, at] + core_recv[m, at]
+                part[1, m, at] = sums
+                return jnp.maximum(top, jnp.max(jnp.abs(sums), axis=0))
+
+            top = lax.fori_loop(0, step_blocks // step_chips, merge, top)
     peak = jnp.max(jnp.max(top, axis=1, keepdims=True), axis=0, keepdims=True)
     peak = jnp.maximum(peak, 1e-30)
     scale_send[...] = jnp.broadcast_to(peak * (1.0 / 32000.0), (1, 128))
@@ -319,24 +322,27 @@
         return sums
 
     total = lax.fori_loop(0, chips // step_adds, add_up, jnp.zeros((8, columns), F32))
-    result_ref[:, :columns] = total
+    total_buf[...] = total
+    modes_out = pltpu.make_async_copy(total_buf, result_hbm, out_sem)
+    modes_out.start()
     square = total * total
     power_0 = jnp.sum(square[:, :128], axis=1, keepdims=True)
     power_1 = jnp.sum(square[:, 128:], axis=1, keepdims=True)
     pow_send[...] = jnp.where(iota((8, 128), 1) == 0, power_0, power_1)
-    pow_recv[chan] = pow_send[...]
+    own_power = pltpu.make_async_copy(pow_send, power_hbm.at[chan], own_sem)
+    own_power.start()
     sends = []
     for i in range(1, nchan):
         peer = lax.rem(chan + i, nchan)
         copy = pltpu.make_async_remote_copy(
-            pow_send, pow_recv.at[chan], pow_s.at[i], pow_r.at[i],
+            pow_send, power_hbm.at[chan], pow_s.at[i], pow_r.at[i],
             device_id={"chan": peer, "pair": me}, device_id_type=MESH)
         copy.start()
         sends.append(copy)
     for copy in sends:
         copy.wait()
-    power = jnp.sum(pow_recv[...], axis=0) * (1.0 / (nchan * sets))
-    result_ref[:, columns:] = power
+    own_power.wait()
+    modes_out.wait()
 
     for copy in to_core:
         copy.wait_send()
@@ -357,12 +363,13 @@
     pltpu.make_async_copy(scale_recv.at[pl.ds(1, chips - 1)], scale_recv.at[pl.ds(1, chips - 1)], scale_s).wait()
 
 
-def shape_results(mwin, sets, result_ref, modes_ref, power_ref):
+def shape_results(mwin, sets, result_ref, powers_ref, modes_ref, power_ref):
     for m in range(mwin):
         for part in range(2):
             at = (2 * m + part) * sets
             modes_ref[:, m, part, :] = result_ref[:, at:at + sets]
-    power_ref[...] = jnp.transpose(result_ref[:, 2 * mwin * sets:])[:mwin]
+    power = jnp.sum(powers_ref[...], axis=0) * (1.0 / (powers_ref.shape[0] * sets))
+    power_ref[...] = jnp.transpose(power)[:mwin]
 
 
 def per_device(visibility, pair_counts, owner_ids, slot_ids, beam):
@@ -373,11 +380,14 @@
     chips = n // 2
     vmem, hbm = pl.BlockSpec(memory_space=pltpu.VMEM), pl.BlockSpec(memory_space=pltpu.HBM)
     dma = pltpu.SemaphoreType.DMA
-    result = pl.pallas_call(
+    amplitudes, powers = pl.pallas_call(
         functools.partial(body, n, nchan, sets),
-        out_shape=jax.ShapeDtypeStruct((8, columns + 128), F32),
+        out_shape=(
+            jax.ShapeDtypeStruct((8, columns), F32),
+            jax.ShapeDtypeStruct((nchan, 8, 128), F32),
+        ),
         in_specs=[hbm] * 5,
-        out_specs=vmem,
+        out_specs=(hbm, hbm),
         scratch_shapes=[
             pltpu.VMEM((1, rows), I32),
             pltpu.VMEM((1, rows), I32),
@@ -399,10 +409,10 @@
             pltpu.VMEM((chips, 8, columns), I16),
             pltpu.VMEM((1, 128), F32),
             pltpu.VMEM((chips, 1, 128), F32),
+            pltpu.VMEM((8, columns), F32),
             pltpu.VMEM((8, 128), F32),
-            pltpu.VMEM((nchan, 8, 128), F32),
-            dma((4,)), dma, dma, dma, dma((nchan,)), dma, dma, dma, dma((mwin,)), dma((mwin,)), dma, dma, dma, dma,
-            dma((nchan,)), dma((nchan,)),
+            dma((4,)), dma, dma, dma, dma((nchan,)), dma, dma, dma, dma((mwin, 2)), dma((mwin, 2)), dma, dma, dma, dma,
+            dma((nchan,)), dma((nchan,)), dma, dma,
         ],
         compiler_params=pltpu.CompilerParams(
             collective_id=0, has_side_effects=True
@@ -415,10 +425,10 @@
     shaped, power = pl.pallas_call(
         functools.partial(shape_results, mwin, sets),
         out_shape=(jax.ShapeDtypeStruct((8, mwin, 2, sets), F32), jax.ShapeDtypeStruct((mwin, 8), F32)),
-        in_specs=[vmem],
+        in_specs=[vmem] * 2,
         out_specs=(vmem, vmem),
         name="shape_results",
-    )(result)
+    )(amplitudes, powers)
     return shaped[None], power.T
 
 

time: 60.3 us -> 57.3 us (0.950)
  Pallas kernels: 59.4 us -> 56.5 us
    pallas_call x1, Pallas kernels: 58 us -> 55.1 us  [per_device(): pl.pallas_call(functools.partial(body, n, nchan, sets), out_shape=(jax.Sh...]
where the time goes in v5:
time: 57.3 us; the launch traced here: 57.1 us
  Pallas kernels  56.5 us (99%)
  between operations  0.64 us (1%)
    pallas_call x1, Pallas kernels, per_device(): pl.pallas_call(functools.partial(body, n, nchan, sets), out_shape=(jax.Sh...  55.1 us
    pallas_call x1, Pallas kernels, per_device(): pl.pallas_call(functools.partial(shape_results, mwin, sets), out_shape=(j...  1.43 us

profile of v5, /device:TPU:1, one launch (start us, length us, event | category | flops | bytes accessed | tf_op | source)
XLA Modules:
  0.0 57.1 jit_solution(17994010861352754857)
XLA Ops:
  0.6 55.1 %stack_project.1 = (f32[8,256]{1,0:T(8,128)}, f32[4,8,128]{2,1,0:T(8,128)}) custom-call(s32[1,512]{1,0:T(1,128)} %bitcast.9, s32[1,512]{1,0:T(1,128)} %bitcast.10, s32[1,512]{1,0:T(1,128)} %bitcast.11, bf16[512,256]{1,0:T(8,128)(2,1)} %bitcast.8, f32[2,2,128,1024]{3,2,1,0:T(8,128)} %bitcast.7), custom_call_target="tpu_custom_call" | custom-call | tf_op jit(solution)/shard_map/stack_project/pallas_call | solution.py:383
  55.7 1.4 %shape_results.1 = (f32[8,2,2,64]{3,2,1,0:T(2,128)}, f32[2,8]{1,0:T(2,128)}) custom-call(f32[8,256]{1,0:T(8,128)} %get-tuple-element.6.result_ref, f32[4,8,128]{2,1,0:T(8,128)} %get-tuple-element.7.powers_ref), custom_call_target="tpu_custom_call" | custom-call | tf_op jit(solution)/shard_map/shape_results/pallas_call | solution.py:425

commit v6 on v5

--- a/solution.py
+++ b/solution.py
@@ -59,14 +59,17 @@
     depth = chips // side
     chip_row, chip_spot = lax.div(chip, side), lax.rem(chip, side)
 
+    turn_sign = 1 - 2 * core
+
     def far(k, size):
         half = lax.div(k, 2) if not isinstance(k, int) else k // 2
-        return size // 2 + half - (k - 2 * half) * (2 * half + 1)
-
-    def each_chip(visit):
+        return size // 2 + turn_sign * (half - (k - 2 * half) * (2 * half + 1))
+
+    def own_row(visit):
         for k in range(side - 1):
             visit(chip_row * side + lax.rem(chip_spot + far(k, side), side))
 
+    def other_rows(visit):
         def diagonal(total, carry):
             def step(k, carry):
                 line = lax.rem(chip_row + far(k, depth), depth)
@@ -77,6 +80,10 @@
 
         lax.fori_loop(0, depth + side - 2, diagonal, 0)
 
+    def each_chip(visit):
+        own_row(visit)
+        other_rows(visit)
+
     def greet(pair):
         pl.semaphore_signal(barrier, inc=1, device_id={"chan": chan, "pair": pair}, device_id_type=MESH)
 
@@ -84,7 +91,8 @@
         greet(peer * 2)
         greet(peer * 2 + 1)
 
-    each_chip(greet_chip)
+    other_rows(greet_chip)
+    own_row(greet_chip)
     greet(chip * 2 + 1 - core)
     for i in range(1, nchan):
         peer = lax.rem(chan + i, nchan)
@@ -222,15 +230,22 @@
 
     slot_a, slot_b = flat(spread[:16], at_a), flat(spread[:16], at_b)
     weight_a, weight_b = flat(spread[16:], at_a), flat(spread[16:], at_b)
-    bases = iota((base, n * 8), 0).astype(F32)
-    first = (iota((base, n * 8), 1) & 4) == 0
-    hit_a = jnp.where(bases == slot_a, 1.0, 0.0)
-    hit_b = jnp.where(bases == slot_b, 1.0, 0.0)
-    hot_a[...] = hit_a.astype(BF16)
-    hot_b[:base] = jnp.where(first, hit_b, 0.0).astype(BF16)
-    hot_b[base:] = jnp.where(first, 0.0, hit_b).astype(BF16)
-    denom = jnp.sum(hit_a * weight_a + jnp.where(first, hit_b, 0.0) * weight_b, axis=1, keepdims=True)
-    bottom[...] = jnp.broadcast_to(jnp.maximum(denom, 1.0), (base, 128))
+    first = (iota((16, n * 8), 1) & 4) == 0
+
+    def mark(i, carry):
+        at = pl.multiple_of(i * 16, 16)
+        bases = (iota((16, n * 8), 0) + at).astype(F32)
+        hit_a = jnp.where(bases == slot_a, 1.0, 0.0)
+        hit_b = jnp.where(bases == slot_b, 1.0, 0.0)
+        hit_0 = jnp.where(first, hit_b, 0.0)
+        hot_a[pl.ds(at, 16)] = hit_a.astype(BF16)
+        hot_b[pl.ds(at, 16)] = hit_0.astype(BF16)
+        hot_b[pl.ds(base + at, 16)] = (hit_b - hit_0).astype(BF16)
+        denom = jnp.sum(hit_a * weight_a + hit_0 * weight_b, axis=1, keepdims=True)
+        bottom[pl.ds(at, 16)] = jnp.broadcast_to(jnp.maximum(denom, 1.0), (16, 128))
+        return carry
+
+    lax.fori_loop(0, base // 16, mark, 0)
 
     pltpu.make_async_copy(recv, recv, data_r).wait()
 

time: 57.3 us -> 57.1 us (level)
  no operation moved by 1% of the time
where the time goes in v6:
time: 57.1 us; the launch traced here: 56.9 us
  Pallas kernels  56.3 us (99%)
  between operations  0.64 us (1%)
    pallas_call x1, Pallas kernels, per_device(): pl.pallas_call(functools.partial(body, n, nchan, sets), out_shape=(jax.Sh...  54.9 us
    pallas_call x1, Pallas kernels, per_device(): pl.pallas_call(functools.partial(shape_results, mwin, sets), out_shape=(j...  1.43 us

profile of v6, /device:TPU:1, one launch (start us, length us, event | category | flops | bytes accessed | tf_op | source)
XLA Modules:
  0.0 56.9 jit_solution(2070637315468153124)
XLA Ops:
  0.6 54.9 %stack_project.1 = (f32[8,256]{1,0:T(8,128)}, f32[4,8,128]{2,1,0:T(8,128)}) custom-call(s32[1,512]{1,0:T(1,128)} %bitcast.9, s32[1,512]{1,0:T(1,128)} %bitcast.10, s32[1,512]{1,0:T(1,128)} %bitcast.11, bf16[512,256]{1,0:T(8,128)(2,1)} %bitcast.8, f32[2,2,128,1024]{3,2,1,0:T(8,128)} %bitcast.7), custom_call_target="tpu_custom_call" | custom-call | tf_op jit(solution)/shard_map/stack_project/pallas_call | solution.py:398
  55.5 1.4 %shape_results.1 = (f32[8,2,2,64]{3,2,1,0:T(2,128)}, f32[2,8]{1,0:T(2,128)}) custom-call(f32[8,256]{1,0:T(8,128)} %get-tuple-element.6.result_ref, f32[4,8,128]{2,1,0:T(8,128)} %get-tuple-element.7.powers_ref), custom_call_target="tpu_custom_call" | custom-call | tf_op jit(solution)/shard_map/shape_results/pallas_call | solution.py:440

commit v7 on v6

--- a/solution.py
+++ b/solution.py
@@ -80,10 +80,6 @@
 
         lax.fori_loop(0, depth + side - 2, diagonal, 0)
 
-    def each_chip(visit):
-        own_row(visit)
-        other_rows(visit)
-
     def greet(pair):
         pl.semaphore_signal(barrier, inc=1, device_id={"chan": chan, "pair": pair}, device_id_type=MESH)
 
@@ -138,6 +134,17 @@
 
     pl.semaphore_wait(barrier, n - 1 + nchan - 1)
 
+    def ship(peer):
+        pltpu.make_async_remote_copy(
+            send.at[peer], recv.at[me], data_s, data_r,
+            device_id={"chan": chan, "pair": peer}, device_id_type=MESH).start()
+
+    def ship_chip(peer):
+        ship(peer * 2 + core)
+        ship(peer * 2 + 1 - core)
+
+    own_row(ship_chip)
+
     def send_meta(pair):
         pltpu.make_async_remote_copy(
             meta_send.at[pair], meta_recv.at[me], meta_s, meta_r,
@@ -147,13 +154,16 @@
     group = lax.div(chip, nchan)
     keeper = lax.rem(chip, nchan) == chan
 
+    at_once = 5 if groups % 5 == 1 else 1
+
     def send_metas(i, carry):
-        peer = lax.rem(group + i, groups) * nchan + chan
-        send_meta(peer * 2)
-        send_meta(peer * 2 + 1)
+        for j in range(at_once):
+            peer = lax.rem(group + i * at_once + (j + 1), groups) * nchan + chan
+            send_meta(peer * 2)
+            send_meta(peer * 2 + 1)
         return carry
 
-    lax.fori_loop(1, groups, send_metas, 0)
+    lax.fori_loop(0, (groups - 1) // at_once, send_metas, 0)
 
     @pl.when(keeper)
     def _():
@@ -165,20 +175,10 @@
         send_meta((group * nchan + chan) * 2)
         send_meta((group * nchan + chan) * 2 + 1)
 
+    other_rows(ship_chip)
+    ship(chip * 2 + 1 - core)
     own_data = pltpu.make_async_copy(send.at[me], recv.at[me], data_r)
     own_data.start()
-
-    def ship(peer):
-        pltpu.make_async_remote_copy(
-            send.at[peer], recv.at[me], data_s, data_r,
-            device_id={"chan": chan, "pair": peer}, device_id_type=MESH).start()
-
-    def ship_chip(peer):
-        ship(peer * 2 + core)
-        ship(peer * 2 + 1 - core)
-
-    each_chip(ship_chip)
-    ship(chip * 2 + 1 - core)
 
     beam_copy.wait()
     mwin, modes = beam_buf.shape[0], beam_buf.shape[3]
@@ -324,7 +324,13 @@
         pltpu.make_async_remote_copy(
             scale_send, scale_recv.at[chip], scale_s, scale_r, device_id=target, device_id_type=MESH).start()
 
-    each_chip(send_red)
+    own_row(send_red)
+    first_of = [lax.rem(chip_row + far(k, depth), depth) * side for k in range(depth)]
+    spots = [lax.rem(chip_spot + far(k, side), side) for k in range(side)]
+    for total in range(depth + side - 2):
+        for k in range(max(0, total - side + 1), min(depth - 1, total + 1)):
+            send_red(first_of[k] + spots[total - k])
+
     pltpu.make_async_copy(scale_recv, scale_recv, scale_r).wait()
     pltpu.make_async_copy(recv2, recv2, red_r).wait()
 

time: 57.1 us -> 59.1 us (1.035); the launches traced: 56.9 us -> 58 us
  Pallas kernels: 56.3 us -> 57.3 us
    pallas_call x1, Pallas kernels: 54.9 us -> 55.9 us  [per_device(): pl.pallas_call(functools.partial(body, n, nchan, sets), out_shape=(jax.Sh...]
where the time goes in v7:
time: 59.1 us; the launch traced here: 58 us
  Pallas kernels  57.3 us (97%)
  between operations  0.64 us (1%)
    pallas_call x1, Pallas kernels, per_device(): pl.pallas_call(functools.partial(body, n, nchan, sets), out_shape=(jax.Sh...  55.9 us
    pallas_call x1, Pallas kernels, per_device(): pl.pallas_call(functools.partial(shape_results, mwin, sets), out_shape=(j...  1.43 us

profile of v7, /device:TPU:1, one launch (start us, length us, event | category | flops | bytes accessed | tf_op | source)
XLA Modules:
  0.0 58.0 jit_solution(18145455680724160609)
XLA Ops:
  0.6 55.9 %stack_project.1 = (f32[8,256]{1,0:T(8,128)}, f32[4,8,128]{2,1,0:T(8,128)}) custom-call(s32[1,512]{1,0:T(1,128)} %bitcast.9, s32[1,512]{1,0:T(1,128)} %bitcast.10, s32[1,512]{1,0:T(1,128)} %bitcast.11, bf16[512,256]{1,0:T(8,128)(2,1)} %bitcast.8, f32[2,2,128,1024]{3,2,1,0:T(8,128)} %bitcast.7), custom_call_target="tpu_custom_call" | custom-call | tf_op jit(solution)/shard_map/stack_project/pallas_call | solution.py:404
  56.5 1.4 %shape_results.1 = (f32[8,2,2,64]{3,2,1,0:T(2,128)}, f32[2,8]{1,0:T(2,128)}) custom-call(f32[8,256]{1,0:T(8,128)} %get-tuple-element.6.result_ref, f32[4,8,128]{2,1,0:T(8,128)} %get-tuple-element.7.powers_ref), custom_call_target="tpu_custom_call" | custom-call | tf_op jit(solution)/shard_map/shape_results/pallas_call | solution.py:446

commit v8 on v7

--- a/solution.py
+++ b/solution.py
@@ -325,11 +325,7 @@
             scale_send, scale_recv.at[chip], scale_s, scale_r, device_id=target, device_id_type=MESH).start()
 
     own_row(send_red)
-    first_of = [lax.rem(chip_row + far(k, depth), depth) * side for k in range(depth)]
-    spots = [lax.rem(chip_spot + far(k, side), side) for k in range(side)]
-    for total in range(depth + side - 2):
-        for k in range(max(0, total - side + 1), min(depth - 1, total + 1)):
-            send_red(first_of[k] + spots[total - k])
+    other_rows(send_red)
 
     pltpu.make_async_copy(scale_recv, scale_recv, scale_r).wait()
     pltpu.make_async_copy(recv2, recv2, red_r).wait()

time: 59.1 us -> 59.1 us (level)
  no operation moved by 1% of the time
where the time goes in v8:
time: 59.1 us; the launch traced here: 58.3 us
  Pallas kernels  57.7 us (98%)
  between operations  0.64 us (1%)
    pallas_call x1, Pallas kernels, per_device(): pl.pallas_call(functools.partial(body, n, nchan, sets), out_shape=(jax.Sh...  56.3 us
    pallas_call x1, Pallas kernels, per_device(): pl.pallas_call(functools.partial(shape_results, mwin, sets), out_shape=(j...  1.43 us

profile of v8, /device:TPU:1, one launch (start us, length us, event | category | flops | bytes accessed | tf_op | source)
XLA Modules:
  0.0 58.3 jit_solution(6208529084016641234)
XLA Ops:
  0.6 56.3 %stack_project.1 = (f32[8,256]{1,0:T(8,128)}, f32[4,8,128]{2,1,0:T(8,128)}) custom-call(s32[1,512]{1,0:T(1,128)} %bitcast.9, s32[1,512]{1,0:T(1,128)} %bitcast.10, s32[1,512]{1,0:T(1,128)} %bitcast.11, bf16[512,256]{1,0:T(8,128)(2,1)} %bitcast.8, f32[2,2,128,1024]{3,2,1,0:T(8,128)} %bitcast.7), custom_call_target="tpu_custom_call" | custom-call | tf_op jit(solution)/shard_map/stack_project/pallas_call | solution.py:400
  56.9 1.4 %shape_results.1 = (f32[8,2,2,64]{3,2,1,0:T(2,128)}, f32[2,8]{1,0:T(2,128)}) custom-call(f32[8,256]{1,0:T(8,128)} %get-tuple-element.6.result_ref, f32[4,8,128]{2,1,0:T(8,128)} %get-tuple-element.7.powers_ref), custom_call_target="tpu_custom_call" | custom-call | tf_op jit(solution)/shard_map/shape_results/pallas_call | solution.py:442

commit v9 on v6

--- a/solution.py
+++ b/solution.py
@@ -147,13 +147,16 @@
     group = lax.div(chip, nchan)
     keeper = lax.rem(chip, nchan) == chan
 
+    at_once = 5 if groups % 5 == 1 else 1
+
     def send_metas(i, carry):
-        peer = lax.rem(group + i, groups) * nchan + chan
-        send_meta(peer * 2)
-        send_meta(peer * 2 + 1)
+        for j in range(at_once):
+            peer = lax.rem(group + i * at_once + (j + 1), groups) * nchan + chan
+            send_meta(peer * 2)
+            send_meta(peer * 2 + 1)
         return carry
 
-    lax.fori_loop(1, groups, send_metas, 0)
+    lax.fori_loop(0, (groups - 1) // at_once, send_metas, 0)
 
     @pl.when(keeper)
     def _():
@@ -324,7 +327,13 @@
         pltpu.make_async_remote_copy(
             scale_send, scale_recv.at[chip], scale_s, scale_r, device_id=target, device_id_type=MESH).start()
 
-    each_chip(send_red)
+    own_row(send_red)
+    first_of = [lax.rem(chip_row + far(k, depth), depth) * side for k in range(depth)]
+    spots = [lax.rem(chip_spot + far(k, side), side) for k in range(side)]
+    for total in range(depth + side - 2):
+        for k in range(max(0, total - side + 1), min(depth - 1, total + 1)):
+            send_red(first_of[k] + spots[total - k])
+
     pltpu.make_async_copy(scale_recv, scale_recv, scale_r).wait()
     pltpu.make_async_copy(recv2, recv2, red_r).wait()
 

time: 57.1 us -> 57.1 us (level)
  no operation moved by 1% of the time
where the time goes in v9:
time: 57.1 us; the launch traced here: 56.9 us
  Pallas kernels  56.3 us (99%)
  between operations  0.64 us (1%)
    pallas_call x1, Pallas kernels, per_device(): pl.pallas_call(functools.partial(body, n, nchan, sets), out_shape=(jax.Sh...  54.8 us
    pallas_call x1, Pallas kernels, per_device(): pl.pallas_call(functools.partial(shape_results, mwin, sets), out_shape=(j...  1.43 us

profile of v9, /device:TPU:1, one launch (start us, length us, event | category | flops | bytes accessed | tf_op | source)
XLA Modules:
  0.0 56.9 jit_solution(12346889998686038612)
XLA Ops:
  0.6 54.8 %stack_project.1 = (f32[8,256]{1,0:T(8,128)}, f32[4,8,128]{2,1,0:T(8,128)}) custom-call(s32[1,512]{1,0:T(1,128)} %bitcast.9, s32[1,512]{1,0:T(1,128)} %bitcast.10, s32[1,512]{1,0:T(1,128)} %bitcast.11, bf16[512,256]{1,0:T(8,128)(2,1)} %bitcast.8, f32[2,2,128,1024]{3,2,1,0:T(8,128)} %bitcast.7), custom_call_target="tpu_custom_call" | custom-call | tf_op jit(solution)/shard_map/stack_project/pallas_call | solution.py:407
  55.5 1.4 %shape_results.1 = (f32[8,2,2,64]{3,2,1,0:T(2,128)}, f32[2,8]{1,0:T(2,128)}) custom-call(f32[8,256]{1,0:T(8,128)} %get-tuple-element.6.result_ref, f32[4,8,128]{2,1,0:T(8,128)} %get-tuple-element.7.powers_ref), custom_call_target="tpu_custom_call" | custom-call | tf_op jit(solution)/shard_map/shape_results/pallas_call | solution.py:449
